TPU v7x, 128 devices: a whole 4x4x4 slice. The times are simulated.
128 devices in a mesh: tgt: 16 (over z, x), src: 8 (over y, core).
Axes of the slice: x: 4, y: 4, z: 4, core: 2. Of those that a mesh axis runs over, the one named last changes fastest.
Arguments:
- points: bfloat16 [262144, 256], P(('tgt', 'src')), may hold values from -0.4 to 0.4
- weights: bfloat16 [262144, 64], P(('tgt', 'src')), may hold values from -6 to 6
- near_list: int32 [2048, 16], P(('tgt', 'src')), may hold values from -1 to 127, as said below
- far_list: int32 [2048, 3, 8], P('tgt', None, 'src'), may hold values from -1 to 63, as said below
- skel_index: int32 [896, 256], P(('tgt', 'src')), may hold values from 0 to 2047, as said below
- equiv_weights: bfloat16 [896, 256, 64], P(('tgt', 'src')), may hold values from -6 to 6
Outputs:
- potential: float32 [262144, 64], P(('tgt', 'src'))
Inputs may be any that keep to these rules, and one draw needn't show every extreme that they name: `near_list`: row b lists blocks of b's group of 128 blocks by their index within the group: first b itself, then distinct other blocks; after a row's live entries all are -1; every row has 4 or more live entries. `far_list`: entry [b, l, c] is -1 or a level-l node owned by a device of src index c, numbered as the owner's tgt index times (16 // (4 * 2 ** l)) plus the node's number among the owner's level-l nodes. `skel_index`: Level-l nodes of a device cover 4 * 128 * 2 ** l consecutive points of that device each, in order; a node's 256 entries are increasing indices of the device's points inside the node.
All inputs are finite; a program needn't handle non-finite values.
Results may differ from a plain program's by a relative error of at most 0.0023.
Values may be sent and summed in bfloat16 or wider, within the bound.
No kernel may reach another device: no remote copies, remote signals or barrier semaphores. Data moves between devices by JAX's collectives and lax.ppermute only.
A program may use at most 192 MiB of HBM per device.

v0:
```python
import jax
import jax.numpy as jnp
from jax import lax
from jax.sharding import PartitionSpec as P

E = 256
WCOL = 64
BLK = 128
RANK = 256
NEAR = 16
LEVELS = 3


kernel_rate = 2.0


def square_norms(values):
    return jnp.sum(jnp.square(values.astype(jnp.float32)), axis=-1)


def tile_kernel(targets, target_norms, sources, source_norms, live_mask):
    dot_terms = jnp.einsum("bie,bse->bis", targets, sources, preferred_element_type=jnp.float32)
    sq_dist = target_norms[:, :, None] + source_norms[:, None, :] - 2.0 * dot_terms
    return jnp.where(live_mask[:, None, :], jnp.exp(-kernel_rate * sq_dist), 0.0).astype(
        jnp.bfloat16
    )


def apply_tile(kernel, source_weights):
    return jnp.einsum("bis,bsw->biw", kernel, source_weights, preferred_element_type=jnp.float32)


def shards(points, weights, near_list, far_list, skel_index, equiv_weights):
    point_dev = points.shape[0]
    blk_dev = point_dev // BLK
    src_size = lax.axis_size("src")
    src_index = lax.axis_index("src")
    group_blocks = src_size * blk_dev
    node_dev = skel_index.shape[0]
    level_nodes = [blk_dev // (4 * 2**tree_level) for tree_level in range(LEVELS)]
    level_start = [sum(level_nodes[:tree_level]) for tree_level in range(LEVELS)]
    group_pts, group_wts = (
        lax.all_gather(points, "src", axis=0, tiled=True),
        lax.all_gather(weights, "src", axis=0, tiled=True),
    )
    tgt_blocks = group_pts.reshape(group_blocks, BLK, E)
    tgt_norms = square_norms(group_pts).reshape(group_blocks, BLK)
    wt_blocks = group_wts.reshape(group_blocks, BLK, WCOL)
    skel_pts = jnp.take(points, skel_index.reshape(-1), axis=0).reshape(node_dev, RANK, E)
    panels = []
    for tree_level in range(LEVELS):
        first_node = level_start[tree_level]
        last_node = first_node + level_nodes[tree_level]
        lvl_pts, lvl_wts = (
            lax.all_gather(skel_pts[first_node:last_node], "tgt", axis=0, tiled=True),
            lax.all_gather(equiv_weights[first_node:last_node], "tgt", axis=0, tiled=True),
        )
        panels.append((lvl_pts, square_norms(lvl_pts), lvl_wts, level_nodes[tree_level], 0))
    own_blocks = points.reshape(blk_dev, BLK, E)
    own_norms = lax.dynamic_slice_in_dim(tgt_norms, src_index * blk_dev, blk_dev, 0)
    near_live = near_list >= 0
    near_index = jnp.where(near_live, near_list, 0)
    sources = tgt_blocks[near_index].reshape(blk_dev, NEAR * BLK, E)
    source_norms = tgt_norms[near_index].reshape(blk_dev, NEAR * BLK)
    source_wts = wt_blocks[near_index].reshape(blk_dev, NEAR * BLK, WCOL)
    kernel = tile_kernel(
        own_blocks, own_norms, sources, source_norms, jnp.repeat(near_live, BLK, axis=1)
    )
    own_near = apply_tile(kernel, source_wts).reshape(point_dev, WCOL)
    row_count = src_size * point_dev
    block_count = row_count // BLK
    far_total = jnp.zeros((block_count, BLK, WCOL), jnp.float32)
    for tree_level in range(LEVELS):
        panel_pts, panel_norms, panel_wts, stride_rows, offset_rows = panels[tree_level]
        level_count = level_nodes[tree_level]
        far_entry = far_list[:, tree_level, 0]
        far_live = far_entry >= 0
        far_entry = jnp.where(far_live, far_entry, 0)
        panel_rows = far_entry // level_count * stride_rows + offset_rows + far_entry % level_count
        kernel = tile_kernel(
            tgt_blocks,
            tgt_norms,
            panel_pts[panel_rows],
            panel_norms[panel_rows],
            jnp.broadcast_to(far_live[:, None], (block_count, RANK)),
        )
        far_total = far_total + apply_tile(kernel, panel_wts[panel_rows])
    whole_term = lax.psum(far_total.reshape(row_count, WCOL), "src")
    mine_term = lax.dynamic_slice_in_dim(whole_term, src_index * point_dev, point_dev, 0)
    mine_term = mine_term + own_near
    return mine_term


def solution(mesh):
    in_specs = (
        P(("tgt", "src"), None),
        P(("tgt", "src"), None),
        P(("tgt", "src"), None),
        P("tgt", None, "src"),
        P(("tgt", "src"), None),
        P(("tgt", "src"), None, None),
    )
    out_specs = P(("tgt", "src"), None)
    return jax.shard_map(shards, mesh=mesh, in_specs=in_specs, out_specs=out_specs, check_vma=False)
```

profile of v0, /device:TPU:0, one launch (start us, length us, event | category | flops | bytes accessed | tf_op | source)
XLA Modules:
  0.0 471.1 jit_solution(658145759099932878)
XLA Ops:
  6.6 1.6 slice.43
  8.2 0.7 all-gather.19.cloned.1.call-update
  9.0 0.7 reshape.304
  9.7 0.7 copy.36
  10.4 5.5 %gather_fusion = bf16[1792,256]{1,0:T(8,128)(2,1)S(1)} fusion(bf16[2048,256]{1,0:T(8,128)(2,1)} %param.6, s32[2048]{0:T(1024)S(1)} %pad_clamp_fusion), kind=kCustom, calls=%fused_computation | custom fusion | bytes 1842176 | tf_op jit(solution)/shard_map/jit(_take)/gather | solution.py:49
  16.0 0.3 broadcast_select_fusion
  16.3 0.7 slice.76
  17.0 0.7 slice.39
  17.8 0.7 slice.75
  18.6 0.5 all-gather.9.cloned.1.call-update
  19.2 0.8 slice.74
  20.1 0.1 reshape.395
  20.2 0.1 broadcast_in_dim.84
  20.4 26.1 %all_gather.30 = bf16[16,256,64]{1,2,0:T(8,128)(2,1)S(1)} all-gather(bf16[1,256,64]{1,2,0:T(8,128)(2,1)S(1)} %slice-done), channel_id=1, replica_groups=mesh['tgt'=16,'src'=8] {'tgt'}, dimensions={0}, use_global_device_ids=true | all-gather | bytes 557056 | tf_op jit(solution)/shard_map/all_gather | solution.py:56
  46.5 2.8 gather_fusion.9
  49.3 5.6 %all-gather.17.cloned.1.call-done = bf16[32,256,64]{1,2,0:T(8,128)(2,1)} async-done(((bf16[2,256,64]{1,2,0:T(8,128)(2,1)}), bf16[32,256,64]{1,2,0:T(8,128)(2,1)}) %all-gather.17.cloned.1.call-update) | async-done | bytes 1048592 | tf_op jit(solution)/shard_map/all_gather | solution.py:56
  54.9 4.0 gather_fusion.6
  58.9 22.5 %all-gather.19.cloned.1.call-done = bf16[16384,64]{0,1:T(8,128)(2,1)} async-done(((bf16[2048,64]{0,1:T(8,128)(2,1)}), bf16[16384,64]{0,1:T(8,128)(2,1)}) %all-gather.19.cloned.1.call-update) | async-done | bytes 2097168 | tf_op jit(solution)/shard_map/all_gather | solution.py:44
  81.4 2.2 copy_bitcast_fusion.1
  83.6 3.1 gather_fusion.12
  86.7 6.9 %copy.25 = bf16[256,128,64]{1,0,2:T(8,128)(2,1)} copy(bf16[256,128,64]{1,2,0:T(8,128)(2,1)} %gather_fusion.12) | data formatting | bytes 8388608 | tf_op jit(solution)/shard_map/gather | solution.py:65
  93.6 7.3 %reshape.311 = bf16[16,2048,64]{1,0,2:T(8,128)(2,1)} reshape(bf16[256,128,64]{1,0,2:T(8,128)(2,1)} %copy.25) | data formatting | bytes 8388608 | tf_op jit(solution)/shard_map/reshape | solution.py:65
  100.9 28.0 %all-gather.21.cloned.1.call-done = bf16[4096,256]{1,0:T(8,128)(2,1)} async-done(((bf16[256,256]{1,0:T(8,128)(2,1)}), bf16[4096,256]{1,0:T(8,128)(2,1)}) %all-gather.21.cloned.1.call-update) | async-done | bytes 2097168 | tf_op jit(solution)/shard_map/all_gather | solution.py:55
  128.9 10.0 %gather_fusion.8 = bf16[128,256,256]{2,1,0:T(8,128)(2,1)} fusion(bf16[16,256,256]{2,1,0:T(8,128)(2,1)} %bitcast.126, s32[1024]{0:T(1024)S(1)} %pad_clamp_fusion.2), kind=kCustom, calls=%fused_computation.8 | custom fusion | bytes 33554944 | tf_op jit(solution)/shard_map/gather | solution.py:83
  138.9 0.6 multiply_reduce_fusion.3
  139.5 0.8 gather_fusion.7
  140.3 34.9 %all-gather.13.cloned.1.call-done = bf16[64,256,64]{1,2,0:T(8,128)(2,1)} async-done(((bf16[4,256,64]{1,2,0:T(8,128)(2,1)}), bf16[64,256,64]{1,2,0:T(8,128)(2,1)}) %all-gather.13.cloned.1.call-update) | async-done | bytes 2097168 | tf_op jit(solution)/shard_map/all_gather | solution.py:56
  175.2 4.4 gather_fusion.3
  179.6 48.4 %all-gather.15.cloned.1.call-done = bf16[32,256,256]{2,1,0:T(8,128)(2,1)} async-done(((bf16[2,256,256]{2,1,0:T(8,128)(2,1)}), bf16[32,256,256]{2,1,0:T(8,128)(2,1)}) %all-gather.15.cloned.1.call-update) | async-done | bytes 4194320 | tf_op jit(solution)/shard_map/all_gather | solution.py:55
  228.0 3.3 multiply_reduce_fusion.2
  231.3 0.8 gather_fusion.4
  232.1 11.1 %gather_fusion.5 = bf16[128,256,256]{2,1,0:T(8,128)(2,1)} fusion(bf16[32,256,256]{2,1,0:T(8,128)(2,1)} %all-gather.15.cloned.1.call-done, s32[1024]{0:T(1024)S(1)} %pad_clamp_fusion.3), kind=kCustom, calls=%fused_computation.5 | custom fusion | bytes 33554944 | tf_op jit(solution)/shard_map/gather | solution.py:83
  243.2 35.7 %all-gather.9.cloned.1.call-done = bf16[16384,256]{1,0:T(8,128)(2,1)} async-done(((bf16[2048,256]{1,0:T(8,128)(2,1)}), bf16[16384,256]{1,0:T(8,128)(2,1)}) %all-gather.9.cloned.1.call-update) | async-done | bytes 8388624 | tf_op jit(solution)/shard_map/all_gather | solution.py:43
  278.8 5.2 %multiply_reduce_fusion.1 = f32[16384]{0:T(1024)S(1)} fusion(bf16[16384,256]{1,0:T(8,128)(2,1)} %all-gather.9.cloned.1.call-done), kind=kLoop, calls=%fused_computation.34 | loop fusion | flops 12566528 | bytes 8454144 | tf_op jit(solution)/shard_map/reduce_sum | solution.py:18
  284.1 0.7 gather_fusion.10
  284.8 12.7 %gather_fusion.11 = bf16[256,128,256]{2,1,0:T(8,128)(2,1)} fusion(bf16[128,128,256]{2,1,0:T(8,128)(2,1)} %bitcast.128, s32[1024]{0:T(1024)S(1)} %pad_clamp_fusion.1), kind=kCustom, calls=%fused_computation.11 | custom fusion | bytes 33555456 | tf_op jit(solution)/shard_map/gather | solution.py:63
  297.5 14.1 %fusion.16 = f32[128,128,64]{1,2,0:T(8,128)} fusion(bf16[128,256,64]{1,2,0:T(8,128)(2,1)} %gather_fusion.9, bf16[128,256,256]{2,1,0:T(8,128)(2,1)} %gather_fusion.8, bf16[128,128,256]{2,1,0:T(8,128)(2,1)} %bitcast.129, f32[128,256]{1,0:T(8,128)S(1)} %gather_fusion.7, f32[128,128]{1,0:T(8,128)S(1)} %bitcast.135, pred[128]{0:T(512)(128)(4,1)S(1)} %get-tuple-element.6), kind=kOutput, calls=%fused_computation.35 | convolution fusion | flops 2709520384 | bytes 33751168 | tf_op jit(solution)/shard_map/bis,bsw->biw/dot_general | solution.py:30
  311.6 14.3 %fusion.17 = f32[128,128,64]{1,2,0:T(8,128)} fusion(bf16[128,256,64]{1,2,0:T(8,128)(2,1)} %gather_fusion.6, bf16[128,256,256]{2,1,0:T(8,128)(2,1)} %gather_fusion.5, bf16[128,128,256]{2,1,0:T(8,128)(2,1)} %bitcast.130, f32[128,256]{1,0:T(8,128)S(1)} %gather_fusion.4, f32[128,128]{1,0:T(8,128)S(1)} %bitcast.136, pred[128]{0:T(512)(128)(4,1)S(1)} %get-tuple-element.7), kind=kOutput, calls=%fused_computation.36 | convolution fusion | flops 2709520384 | bytes 33751168 | tf_op jit(solution)/shard_map/bis,bsw->biw/dot_general | solution.py:30
  325.9 26.2 %all-gather.11.cloned.1.call-done = bf16[64,256,256]{2,1,0:T(8,128)(2,1)} async-done(((bf16[4,256,256]{2,1,0:T(8,128)(2,1)}), bf16[64,256,256]{2,1,0:T(8,128)(2,1)}) %all-gather.11.cloned.1.call-update) | async-done | bytes 8388624 | tf_op jit(solution)/shard_map/all_gather | solution.py:55
  352.1 5.6 %multiply_reduce_fusion = f32[64,256]{1,0:T(8,128)S(1)} fusion(bf16[64,256,256]{2,1,0:T(8,128)(2,1)} %all-gather.11.cloned.1.call-done), kind=kLoop, calls=%fused_computation.33 | loop fusion | flops 12566528 | bytes 8454144 | tf_op jit(solution)/shard_map/reduce_sum | solution.py:18
  357.7 0.8 gather_fusion.1
  358.5 11.7 %gather_fusion.2 = bf16[128,256,256]{2,1,0:T(8,128)(2,1)} fusion(bf16[64,256,256]{2,1,0:T(8,128)(2,1)} %all-gather.11.cloned.1.call-done, s32[1024]{0:T(1024)S(1)} %pad_clamp_fusion.4), kind=kCustom, calls=%fused_computation.2 | custom fusion | bytes 33554944 | tf_op jit(solution)/shard_map/gather | solution.py:83
  370.2 15.5 %add_bitcast_fusion = f32[128,8,8,128]{3,2,1,0:T(8,128)} fusion(f32[128,128,64]{1,2,0:T(8,128)} %fusion.16, f32[128,128,64]{1,2,0:T(8,128)} %fusion.17, bf16[128,256,64]{1,2,0:T(8,128)(2,1)} %gather_fusion.3, bf16[128,256,256]{2,1,0:T(8,128)(2,1)} %gather_fusion.2, bf16[128,128,256]{2,1,0:T(8,128)(2,1)} %bitcast.131, f32[128,256]{1,0:T(8,128)S(1)} %gather_fusion.1, ...), kind=kOutput, calls=%fused_computation.62 | convolution fusion | flops 2711617536 | bytes 42139776 | tf_op jit(solution)/shard_map/bis,bsw->biw/dot_general | solution.py:30
  385.7 4.5 copy.47
  390.3 12.0 %fusion.87 = bf16[16,128,2048]{1,2,0:T(8,128)(2,1)S(1)} fusion(f32[16,2048]{1,0:T(8,128)S(1)} %add.225, f32[16,128]{1,0:T(8,128)S(1)} %constant_dynamic-slice_fusion, pred[16,2048]{1,0:T(8,128)(4,1)S(1)} %bitcast.143, bf16[16,2048,256]{2,1,0:T(8,128)(2,1)} %bitcast.138, bf16[16,128,256]{2,1,0:T(8,128)(2,1)S(1)} %bitcast.132), kind=kOutput, calls=%fused_computation.17.clone.clone.clone.clone.1 | convolution fusion | flops 2172649472 | bytes 26386432 | tf_op jit(solution)/shard_map/bie,bse->bis/dot_general | solution.py:22
  402.3 5.0 %fusion.43 = f32[16,8,8,128]{3,2,1,0:T(8,128)S(1)} fusion(bf16[16,2048,64]{1,0,2:T(8,128)(2,1)S(1)} %copy-done.2, bf16[16,128,2048]{1,2,0:T(8,128)(2,1)S(1)} %fusion.87), kind=kOutput, calls=%fused_computation.65 | convolution fusion | flops 536870912 | bytes 13107200 | tf_op jit(solution)/shard_map/bis,bsw->biw/dot_general | solution.py:30
  407.3 55.1 %all-reduce.2.cloned.1.call-done = f32[16384,64]{0,1:T(8,128)} async-done(((f32[16384,64]{0,1:T(8,128)}), f32[16384,64]{0,1:T(8,128)}) %all-reduce.2.cloned.1.call-update) | async-done | bytes 4194320 | tf_op jit(solution)/shard_map/psum | solution.py:88
  462.3 1.9 bitcast_add_fusion
  (42 shorter events, 0.6 us)
Async XLA Ops:
  6.5 10.5 %copy-start.3 = (bf16[7,256,64]{1,2,0:T(8,128)(2,1)S(1)}, bf16[7,256,64]{1,2,0:T(8,128)(2,1)}, u32[]{:S(2)}) copy-start(bf16[7,256,64]{1,2,0:T(8,128)(2,1)} %param.11) | copy-start | bytes 688132
  6.5 13.8 %slice-start = ((bf16[7,256,64]{1,2,0:T(8,128)(2,1)}), bf16[1,256,64]{1,2,0:T(8,128)(2,1)S(1)}, s32[]{:S(2)}) async-start(bf16[7,256,64]{1,2,0:T(8,128)(2,1)} %param.11), calls=%async_computation.8 | async-start | bytes 65536 | tf_op jit(solution)/shard_map/slice | solution.py:56
  6.5 13.5 %copy-start.4 = (s32[16,16]{1,0:T(8,128)S(1)}, s32[16,16]{1,0:T(8,128)}, u32[]{:S(2)}) copy-start(s32[16,16]{1,0:T(8,128)} %param.8) | copy-start | bytes 3076
  6.5 13.8 %copy-start.5 = (s32[128,3,1]{0,2,1:T(1,128)S(1)}, s32[128,3,1]{0,2,1:T(1,128)}, u32[]{:S(2)}) copy-start(s32[128,3,1]{0,2,1:T(1,128)} %param.9) | copy-start | bytes 4612
  6.5 48.4 %all-gather.17.cloned.1.call-start = ((), (), s32[]{:S(2)}) async-start(), calls=%async_computation.4 | async-start | bytes 1114112 | tf_op jit(solution)/shard_map/all_gather | solution.py:56
  8.2 73.2 %all-gather.19.cloned.1.call-start = ((), (), s32[]{:S(2)}) async-start(), calls=%async_computation.6 | async-start | bytes 2359296 | tf_op jit(solution)/shard_map/all_gather | solution.py:44
  8.9 120.0 %all-gather.21.cloned.1.call-start = ((), (), s32[]{:S(2)}) async-start(), calls=%async_computation.7 | async-start | bytes 2228224 | tf_op jit(solution)/shard_map/all_gather | solution.py:55
  17.0 158.2 %all-gather.13.cloned.1.call-start = ((), (), s32[]{:S(2)}) async-start(), calls=%async_computation.2 | async-start | bytes 2228224 | tf_op jit(solution)/shard_map/all_gather | solution.py:56
  17.7 210.3 %all-gather.15.cloned.1.call-start = ((), (), s32[]{:S(2)}) async-start(), calls=%async_computation.3 | async-start | bytes 4456448 | tf_op jit(solution)/shard_map/all_gather | solution.py:55
  18.6 260.3 %all-gather.9.cloned.1.call-start = ((), (), s32[]{:S(2)}) async-start(), calls=%async_computation | async-start | bytes 9437184 | tf_op jit(solution)/shard_map/all_gather | solution.py:43
  19.1 333.0 %all-gather.11.cloned.1.call-start = ((), (), s32[]{:S(2)}) async-start(), calls=%async_computation.1 | async-start | bytes 8912896 | tf_op jit(solution)/shard_map/all_gather | solution.py:55
  20.0 442.3 %all-reduce.2.cloned.1.call-start = ((), (), s32[]{:S(2)}) async-start(), calls=%async_computation.5 | async-start | bytes 8388608 | tf_op jit(solution)/shard_map/psum | solution.py:88
  128.9 10.0 %copy-start = (bf16[4096,256]{1,0:T(8,128)(2,1)S(1)}, bf16[4096,256]{1,0:T(8,128)(2,1)}, u32[]{:S(2)}) copy-start(bf16[4096,256]{1,0:T(8,128)(2,1)} %all-gather.21.cloned.1.call-done) | copy-start | bytes 6291460
  385.7 4.5 copy-start.1
  390.3 12.0 %copy-start.2 = (bf16[16,2048,64]{1,0,2:T(8,128)(2,1)S(1)}, bf16[16,2048,64]{1,0,2:T(8,128)(2,1)}, u32[]{:S(2)}) copy-start(bf16[16,2048,64]{1,0,2:T(8,128)(2,1)} %reshape.311) | copy-start | bytes 12582916
Sparse Core Ops, SparseCore 0:
  9.5 45.4 all-gather.16
  56.6 24.7 all-gather.18
  83.6 45.3 all-gather.20
  130.9 44.2 all-gather.12
  177.2 50.7 all-gather.14
  229.6 49.2 all-gather.8
  281.0 71.0 all-gather.10
  390.4 71.9 all-reduce.1
where the time goes:
time: 472 us; the launch traced here: 471 us
  waiting for transfers between devices  258 us (55%)
  local copies, waits for them, and re-layouts  95.3 us (20%)
  matrix products  60.9 us (13%)
  blocking collectives  26.1 us (6%)
  other arithmetic  17.1 us (4%)
  between operations  13.7 us (3%)
    all_gather x3, waiting for transfers between devices, shards(): lax.all_gather(skel_pts[first_node:last_node], 'tgt', axis=0, tiled=True)  103 us
    psum x1, waiting for transfers between devices, shards(): whole_term = lax.psum(far_total.reshape(row_count, WCOL), 'src')  55.1 us
    dot_general x4, matrix products, apply_tile(): jnp.einsum('bis,bsw->biw', kernel, source_weights, preferred_element_type...  49 us
    all_gather x2, waiting for transfers between devices, shards(): lax.all_gather(equiv_weights[first_node:last_node], 'tgt', axis=0, tiled=...  40.5 us
    all_gather x1, waiting for transfers between devices, shards(): lax.all_gather(points, 'src', axis=0, tiled=True)  35.7 us
    gather x3, local copies, waits for them, and re-layouts, shards(): panel_pts[panel_rows]  32.8 us
    all_gather x1, blocking collectives, shards(): lax.all_gather(equiv_weights[first_node:last_node], 'tgt', axis=0, tiled=...  26.1 us
    all_gather x1, waiting for transfers between devices, shards(): lax.all_gather(weights, 'src', axis=0, tiled=True)  22.5 us
  transfers between devices with their start and end apart: 8, of which 8 were waited for; matrix products, arithmetic and copies ran while one was open for 28% of the time, Pallas kernels for 0%

commit v1 on v0

v1 whole, which is shorter than its diff:
```python
import jax
import jax.numpy as jnp
from jax import lax
from jax.experimental import pallas as pl
from jax.experimental.pallas import tpu as pltpu
from jax.sharding import PartitionSpec as P

E = 256
WCOL = 64
BLK = 128
RANK = 256
NEAR = 16
BLK_DEV = 16
PTS = BLK_DEV * BLK
PACK = PTS + BLK_DEV * 32
NODE = RANK + WCOL
LOG2E = 1.4426950408889634
DOT_SCALE = 4.0 * LOG2E
NORM_SCALE = 2.0 * LOG2E
DEAD = 1e30
STEP = 4
F32 = jnp.float32
BF16 = jnp.bfloat16
NT = (((1,), (1,)), ((), ()))


def prep_body(pts, wts, ewts, idx, y_out, l0_out, l12_out):
    y_out[0:PTS, :] = pts[...]
    for b in range(BLK_DEV):
        w = wts[:, b * BLK : (b + 1) * BLK]
        row = PTS + b * 32
        y_out[row : row + 32, 0:BLK] = w[0:32]
        y_out[row : row + 32, BLK:E] = w[32:64]

    def node(r, first, size, out, slot):
        iota = lax.broadcasted_iota(jnp.int32, (RANK, size), 1)
        pick = jnp.where(iota == idx[:, r : r + 1] - first, 1.0, 0.0).astype(BF16)
        rows = lax.dot_general(pick, pts[first : first + size, :], (((1,), (0,)), ((), ())), preferred_element_type=F32)
        out[slot * NODE : slot * NODE + RANK, :] = rows.astype(BF16)
        out[slot * NODE + RANK : (slot + 1) * NODE, :] = ewts[r]

    node(4, 0, 1024, l12_out, 0)
    node(5, 1024, 1024, l12_out, 1)
    node(6, 0, 2048, l12_out, 2)
    for r in range(4):
        node(r, r * 512, 512, l0_out, r)


def prep(points, weights_t, equiv_t, skel_t):
    return pl.pallas_call(
        prep_body,
        out_shape=(
            jax.ShapeDtypeStruct((PACK, E), BF16),
            jax.ShapeDtypeStruct((4 * NODE, E), BF16),
            jax.ShapeDtypeStruct((3 * NODE, E), BF16),
        ),
        cost_estimate=pl.CostEstimate(flops=10**9, bytes_accessed=8 * 10**6, transcendentals=0),
        name="prep",
    )(points, weights_t, equiv_t, skel_t)


def row_norms(x):
    v = x.astype(F32)
    sq = v * v
    half = sq[:, 0:128] + sq[:, 128:256]
    parts = [jnp.sum(half[i : i + 128].T, axis=0, keepdims=True) for i in range(0, x.shape[0], 128)]
    row = parts[0] if len(parts) == 1 else jnp.concatenate(parts, axis=1)
    return row * NORM_SCALE


def column_of(row):
    col = jnp.broadcast_to(row, (128, 128)).T
    return jnp.concatenate([col, col], axis=1)


def tile(x, col, src, src_row, wt):
    dot = lax.dot_general(x, src, NT, preferred_element_type=F32)
    k = jnp.exp2(dot * DOT_SCALE - col - src_row).astype(BF16)
    return lax.dot_general(wt, k, NT, preferred_element_type=F32)


def near_body(inv, near, *refs):
    pieces = refs[:8]
    x_out, norm_out, near_out, xs, sems, out_sems = refs[8:]

    def load(k):
        return pltpu.make_async_copy(pieces[k], xs.at[pl.ds(k * PACK, PACK), :], sems.at[k])

    def store(k):
        return pltpu.make_async_copy(xs.at[pl.ds(k * PACK, PTS), :], x_out.at[k], out_sems.at[k])

    for k in range(8):
        load(k).start()
    for k in range(8):
        load(k).wait()
        store(k).start()

        def norms(q, carry, k=k):
            for u in range(4):
                i = q * 4 + u
                x = xs[pl.ds(pl.multiple_of(k * PACK + i * BLK, BLK), BLK), :]
                norm_out[pl.ds(k * BLK_DEV + i, 1), :] = row_norms(x)
            return carry

        lax.fori_loop(0, BLK_DEV // 4, norms, 0)

    def block(i, carry):
        x = xs[pl.ds(pl.multiple_of(i * BLK, BLK), BLK), :]
        col = column_of(norm_out[pl.ds(i, 1), :])
        acc = None
        for pair in range(NEAR // 2):
            srcs, rows, wts = [], [], []
            for s in range(2):
                v = near[i * NEAR + pair * 2 + s]
                j = jnp.maximum(v, 0)
                k = inv[j // BLK_DEV]
                i2 = j % BLK_DEV
                srcs.append(xs[pl.ds(pl.multiple_of(k * PACK + i2 * BLK, BLK), BLK), :])
                bias = jnp.where(v >= 0, 0.0, DEAD).astype(F32)
                rows.append(norm_out[pl.ds(k * BLK_DEV + i2, 1), :] + bias)
                w = xs[pl.ds(pl.multiple_of(k * PACK + PTS + i2 * 32, 32), 32), :]
                wts.append(jnp.concatenate([w[:, 0:128], w[:, 128:256]], axis=0))
            part = tile(x, col, jnp.concatenate(srcs, axis=0), jnp.concatenate(rows, axis=1), jnp.concatenate(wts, axis=1))
            acc = part if acc is None else acc + part
        near_out[i] = acc
        return carry

    lax.fori_loop(0, BLK_DEV, block, 0)
    for k in range(8):
        store(k).wait()


def near_call(inv, near_list, pieces):
    anys = pl.BlockSpec(memory_space=pl.ANY)
    vm = pl.BlockSpec(memory_space=pltpu.VMEM)
    return pl.pallas_call(
        near_body,
        grid_spec=pltpu.PrefetchScalarGridSpec(
            num_scalar_prefetch=2,
            grid=(),
            in_specs=[anys] * 8,
            out_specs=(anys, vm, vm),
            scratch_shapes=[
                pltpu.VMEM((8 * PACK, E), BF16),
                pltpu.SemaphoreType.DMA((8,)),
                pltpu.SemaphoreType.DMA((8,)),
            ],
        ),
        out_shape=(
            jax.ShapeDtypeStruct((8, PTS, E), BF16),
            jax.ShapeDtypeStruct((8 * BLK_DEV, BLK), F32),
            jax.ShapeDtypeStruct((BLK_DEV, WCOL, BLK), F32),
        ),
        cost_estimate=pl.CostEstimate(flops=6 * 10**9, bytes_accessed=20 * 10**6, transcendentals=4 * 10**6),
        name="near",
    )(inv, near_list, *pieces)


def far_call(name, slots, far, x_all, norms, panel, places, acc):
    levels = len(places)
    panel_nodes = panel.shape[0] // NODE
    steps = 8 * BLK_DEV // STEP
    per_slot = BLK_DEV // STEP

    def body(slots, far, *refs):
        if acc is None:
            x_ref, norm_ref, panel_hbm, out_ref, pan, node_norms, sem = refs
        else:
            x_ref, norm_ref, panel_hbm, acc_ref, out_ref, pan, node_norms, sem = refs
        step = pl.program_id(0)

        @pl.when(step == 0)
        def _():
            copy = pltpu.make_async_copy(panel_hbm, pan, sem)
            copy.start()
            copy.wait()

            def norms_of(q, carry):
                for u in range(4):
                    n = q * 4 + u
                    x = pan[pl.ds(pl.multiple_of(n * NODE, NODE), RANK), :]
                    node_norms[pl.ds(n, 1), :] = row_norms(x)
                return carry

            lax.fori_loop(0, panel_nodes // 4, norms_of, 0)

        k = step // per_slot
        first = (step % per_slot) * STEP
        for u in range(STEP):
            x = x_ref[0, u * BLK : (u + 1) * BLK, :]
            col = column_of(norm_ref[pl.ds(step * STEP + u, 1), :])
            total = None if acc is None else acc_ref[0, u]
            for level in range(levels):
                v = far[(slots[k] * BLK_DEV + first + u) * levels + level]
                n = places[level](jnp.maximum(v, 0))
                row = pl.multiple_of(n * NODE, NODE)
                bias = jnp.where(v >= 0, 0.0, DEAD).astype(F32)
                part = tile(
                    x,
                    col,
                    pan[pl.ds(row, RANK), :],
                    node_norms[pl.ds(n, 1), :] + bias,
                    pan[pl.ds(row + RANK, WCOL), :],
                )
                total = part if total is None else total + part
            out_ref[0, u] = total

    blocked = pl.BlockSpec((1, STEP, WCOL, BLK), lambda s, *_: (s // per_slot, s % per_slot, 0, 0))
    in_specs = [
        pl.BlockSpec((1, STEP * BLK, E), lambda s, *_: (s // per_slot, s % per_slot, 0)),
        pl.BlockSpec((8 * BLK_DEV, BLK), lambda s, *_: (0, 0)),
        pl.BlockSpec(memory_space=pl.ANY),
    ]
    operands = [x_all, norms, panel]
    if acc is not None:
        in_specs.append(blocked)
        operands.append(acc)
    return pl.pallas_call(
        body,
        grid_spec=pltpu.PrefetchScalarGridSpec(
            num_scalar_prefetch=2,
            grid=(steps,),
            in_specs=in_specs,
            out_specs=blocked,
            scratch_shapes=[
                pltpu.VMEM(panel.shape, BF16),
                pltpu.VMEM((panel_nodes, RANK), F32),
                pltpu.SemaphoreType.DMA,
            ],
        ),
        out_shape=jax.ShapeDtypeStruct((8, BLK_DEV, WCOL, BLK), F32),
        cost_estimate=pl.CostEstimate(
            flops=levels * 5 * 10**9, bytes_accessed=25 * 10**6, transcendentals=levels * 4 * 10**6
        ),
        name=name,
    )(slots, far, *operands)


def shards(points, weights, near_list, far_list, skel_index, equiv_weights):
    src_index = lax.axis_index("src")
    y_size = lax.axis_size("src") // 2

    def along_y(d):
        return [(s, ((s // 2 + d) % y_size) * 2 + s % 2) for s in range(2 * y_size)]

    partner = [(s, s ^ 1) for s in range(2 * y_size)]

    def shift(v, d):
        return lax.ppermute(v, "src", along_y(d))

    def swap(v):
        return lax.ppermute(v, "src", partner)

    y, core = src_index // 2, src_index % 2
    ys = [(y + d) % y_size for d in (0, -1, 1, 2)]
    slots = jnp.stack([ys[d] * 2 + (core ^ f) for f in range(2) for d in range(4)])
    inv = jnp.sum(jnp.where(slots[:, None] == jnp.arange(8)[None, :], jnp.arange(8)[:, None], 0), axis=0)
    slots, inv = slots.astype(jnp.int32), inv.astype(jnp.int32)

    pack, l0, l12 = prep(points, weights.T, jnp.swapaxes(equiv_weights, 1, 2), skel_index.T)
    mine = [pack, shift(pack, 1), shift(pack, -1), shift(pack, 2)]
    pieces = mine + [swap(v) for v in mine]
    panel12 = lax.all_gather(l12, "tgt", axis=0, tiled=True)
    panel0 = lax.all_gather(l0, "tgt", axis=0, tiled=True)

    x_all, norms, near_sum = near_call(inv, near_list.reshape(-1), pieces)
    far = far_list[:, :, 0]
    places12 = (lambda v: (v // 2) * 3 + v % 2, lambda v: v * 3 + 2)
    far12 = far_call("far12", slots, far[:, 1:].reshape(-1), x_all, norms, panel12, places12, None)
    total = far_call("far0", slots, far[:, 0].reshape(-1), x_all, norms, panel0, (lambda v: v,), far12)

    chip = total[0:4] + swap(total[4:8].astype(BF16)).astype(F32)
    got = [
        shift(chip[1].astype(BF16), -1),
        shift(chip[2].astype(BF16), 1),
        shift(chip[3].astype(BF16), 2),
    ]
    out = near_sum + chip[0]
    for g in got:
        out = out + g.astype(F32)
    return out.transpose(0, 2, 1).reshape(PTS, WCOL)


def solution(mesh):
    in_specs = (
        P(("tgt", "src"), None),
        P(("tgt", "src"), None),
        P(("tgt", "src"), None),
        P("tgt", None, "src"),
        P(("tgt", "src"), None),
        P(("tgt", "src"), None, None),
    )
    out_specs = P(("tgt", "src"), None)
    return jax.shard_map(shards, mesh=mesh, in_specs=in_specs, out_specs=out_specs, check_vma=False)
```

time: 472 us -> 242 us (0.51)
  waiting for transfers between devices: 258 us -> 88.1 us
  Pallas kernels: 0 us -> 119 us
  local copies, waits for them, and re-layouts: 95.3 us -> 5.5 us
  matrix products: 60.9 us -> 0 us
  blocking collectives: 26.1 us -> 0 us
  other arithmetic: 17.1 us -> 3.65 us
  starting transfers between devices: 0.32 us -> 10.8 us
    all_gather x7 -> x2, waiting for transfers between devices: 201 us -> 17.6 us  [the longest x1 17.6 us: shards(): panel0 = lax.all_gather(l0, 'tgt', axis=0, tiled=True)]
    pallas_call x0 -> x4, Pallas kernels: none -> 119 us  [the longest x2 92.8 us: far_call(): pl.pallas_call(body, grid_spec=pltpu.PrefetchScalarGridSpec(num_scalar_pr...]
    gather x14 -> x0, local copies, waits for them, and re-layouts: 75.1 us -> none  [the longest x3 32.8 us: shards(): panel_pts[panel_rows]]
    ppermute x0 -> x11, waiting for transfers between devices: none -> 69.8 us  [the longest x6 66.6 us: shift(): return lax.ppermute(v, 'src', along_y(d))]
    dot_general x5 -> x0, matrix products: 60.9 us -> none  [the longest x4 49 us: apply_tile(): jnp.einsum('bis,bsw->biw', kernel, source_weights, preferred_element_type...]
    psum x1 -> x0, waiting for transfers between devices: 55.1 us -> none  [shards(): whole_term = lax.psum(far_total.reshape(row_count, WCOL), 'src')]
    all_gather x1 -> x0, blocking collectives: 26.1 us -> none  [shards(): lax.all_gather(equiv_weights[first_node:last_node], 'tgt', axis=0, tiled=...]
    reduce_sum x4 -> x1, other arithmetic: 14.8 us -> 0.68 us  [shards(): jnp.sum(jnp.where(slots[:, None] == jnp.arange(8)[None, :], jnp.arange(8)...]
  transfers between devices with their start and end apart: 8 -> 13, of which waited for: 8 -> 8; matrix products, arithmetic and copies ran while one was open for 28% -> 1% of each run, Pallas kernels for 0% -> 29%
where the time goes in v1:
time: 242 us; the launch traced here: 240 us
  Pallas kernels  119 us (49%)
  waiting for transfers between devices  88.1 us (36%)
  between operations  13.5 us (6%)
  starting transfers between devices  10.8 us (4%)
  local copies, waits for them, and re-layouts  5.5 us (2%)
  other arithmetic  3.65 us (2%)
    pallas_call x2, Pallas kernels, far_call(): pl.pallas_call(body, grid_spec=pltpu.PrefetchScalarGridSpec(num_scalar_pr...  92.8 us
    ppermute x6, waiting for transfers between devices, shift(): return lax.ppermute(v, 'src', along_y(d))  66.6 us
    pallas_call x1, Pallas kernels, near_call(): pl.pallas_call(near_body, grid_spec=pltpu.PrefetchScalarGridSpec(num_scal...  22.2 us
    all_gather x1, waiting for transfers between devices, shards(): panel0 = lax.all_gather(l0, 'tgt', axis=0, tiled=True)  17.6 us
    ppermute x6, starting transfers between devices, shift(): return lax.ppermute(v, 'src', along_y(d))  10.6 us
  transfers between devices with their start and end apart: 13, of which 8 were waited for; matrix products, arithmetic and copies ran while one was open for 1% of the time, Pallas kernels for 29%

profile of v1, /device:TPU:0, one launch (start us, length us, event | category | flops | bytes accessed | tf_op | source)
XLA Modules:
  0.0 240.4 jit_solution(4364560939750006378)
XLA Ops:
  6.5 0.0 all-gather.5.cloned.1.call-start
  6.5 1.5 copy.11
  8.0 3.9 %prep.1 = (bf16[2560,256]{1,0:T(8,128)(2,1)}, bf16[1280,256]{1,0:T(8,128)(2,1)}, bf16[960,256]{1,0:T(8,128)(2,1)}) custom-call(bf16[2048,256]{1,0:T(8,128)(2,1)} %pts.1, bf16[64,2048]{1,0:T(8,128)(2,1)} %bitcast.44, bf16[7,64,256]{2,1,0:T(8,128)(2,1)} %bitcast.45, s32[256,7]{1,0:T(8,128)} %bitcast.41), custom_call_target="tpu_custom_call" | custom-call | flops 1000000000 | bytes 8000000 | tf_op jit(solution)/shard_map/prep/pallas_call | solution.py:50
  11.9 0.0 all-gather.5.cloned.1.call-update
  12.0 0.0 all-gather.3.cloned.1.call-start
  12.0 0.7 all-gather.3.cloned.1.call-update
  12.7 1.8 collective-permute-start
  14.5 1.5 collective-permute-start.1
  16.0 2.1 collective-permute-start.2
  18.1 0.0 collective-permute-start.3
  18.1 26.8 %collective-permute-done.refs_1_ = bf16[2560,256]{1,0:T(8,128)(2,1)S(1)} collective-permute-done((bf16[2560,256]{1,0:T(8,128)(2,1)}, bf16[2560,256]{1,0:T(8,128)(2,1)S(1)}, u32[]{:S(2)}, u32[]{:S(2)}) %collective-permute-start) | collective-permute-done | bytes 1310752 | tf_op jit(solution)/shard_map/ppermute | solution.py:249
  44.9 0.0 collective-permute-start.4
  44.9 27.6 %collective-permute-done.1.refs_2_ = bf16[2560,256]{1,0:T(8,128)(2,1)S(1)} collective-permute-done((bf16[2560,256]{1,0:T(8,128)(2,1)}, bf16[2560,256]{1,0:T(8,128)(2,1)S(1)}, u32[]{:S(2)}, u32[]{:S(2)}) %collective-permute-start.1) | collective-permute-done | bytes 1310752 | tf_op jit(solution)/shard_map/ppermute | solution.py:249
  72.5 0.0 collective-permute-start.5
  72.5 1.8 collective-permute-done.2.refs_3_
  74.3 0.0 collective-permute-start.6
  74.3 0.0 copy-done.1
  74.3 0.7 reshape.13.near
  74.9 0.0 copy-done.3
  74.9 0.1 copy.12
  75.1 0.7 reshape.14.far
  75.8 0.1 stack.35.slots
  75.9 0.7 select_reduce_fusion.inv
  76.5 0.6 slice_bitcast_fusion.4.far
  77.1 0.0 collective-permute-done.3.refs_4_
  77.1 0.0 collective-permute-done.4.refs_5_
  77.1 0.0 collective-permute-done.5.refs_6_
  77.1 0.5 collective-permute-done.6.refs_7_
  77.6 0.0 copy-done.4
  77.6 0.0 copy-done.5
  77.6 22.2 %near.1 = (bf16[8,2048,256]{2,1,0:T(8,128)(2,1)}, f32[128,128]{1,0:T(8,128)}, f32[16,64,128]{2,1,0:T(8,128)}) custom-call(s32[8]{0:T(128)} %select_reduce_fusion.inv, s32[256]{0:T(256)} %reshape.13.near, bf16[2560,256]{1,0:T(8,128)(2,1)} %get-tuple-element.11.refs_0_, bf16[2560,256]{1,0:T(8,128)(2,1)} %copy-done.4, bf16[2560,256]{1,0:T(8,128)(2,1)} %copy-done.5, ...), custom_call_target="tpu_custom_call" | custom-call | flops 6000000000 | bytes 20000000 | tf_op jit(solution)/shard_map/near/pallas_call | solution.py:136
  99.8 0.0 all-gather.5.cloned.1.call-done.refs_2_
  99.9 48.0 %far12.1.refs_3_ = f32[8,16,64,128]{3,2,1,0:T(8,128)} custom-call(s32[8]{0:T(128)} %copy-done.2, s32[256]{0:T(256)} %reshape.14.far, bf16[8,2048,256]{2,1,0:T(8,128)(2,1)} %get-tuple-element.13.refs_0_, f32[128,128]{1,0:T(8,128)} %get-tuple-element.14.refs_1_, bf16[15360,256]{1,0:T(8,128)(2,1)} %all-gather.5.cloned.1.call-done.refs_2_), custom_call_target="tpu_custom_call" | custom-call | flops 10000000000 | bytes 25000000 | tf_op jit(solution)/shard_map/far12/pallas_call | solution.py:218
  147.9 17.6 %all-gather.3.cloned.1.call-done.refs_2_ = bf16[20480,256]{1,0:T(8,128)(2,1)} async-done(((bf16[1280,256]{1,0:T(8,128)(2,1)}), bf16[20480,256]{1,0:T(8,128)(2,1)}) %all-gather.3.cloned.1.call-update) | async-done | bytes 10485776 | tf_op jit(solution)/shard_map/all_gather | solution.py:264
  165.4 44.8 %far0.1 = f32[8,16,64,128]{3,2,1,0:T(8,128)} custom-call(s32[8]{0:T(128)} %copy-done.2, s32[128]{0:T(128)} %slice_bitcast_fusion.4.far, bf16[8,2048,256]{2,1,0:T(8,128)(2,1)} %get-tuple-element.13.refs_0_, f32[128,128]{1,0:T(8,128)} %get-tuple-element.14.refs_1_, bf16[20480,256]{1,0:T(8,128)(2,1)} %all-gather.3.cloned.1.call-done.refs_2_, ...), custom_call_target="tpu_custom_call" | custom-call | flops 5000000000 | bytes 25000000 | tf_op jit(solution)/shard_map/far0/pallas_call | solution.py:218
  210.2 1.8 slice.59
  212.0 0.0 copy-start
  212.0 0.1 collective-permute-start.7
  212.1 2.6 %collective-permute-done.7 = bf16[4,16,64,128]{3,2,1,0:T(8,128)(2,1)S(1)} collective-permute-done((bf16[4,16,64,128]{3,2,1,0:T(8,128)(2,1)S(1)}, bf16[4,16,64,128]{3,2,1,0:T(8,128)(2,1)S(1)}, u32[]{:S(2)}, u32[]{:S(2)}) %collective-permute-start.7) | collective-permute-done | bytes 1048608 | tf_op jit(solution)/shard_map/ppermute | solution.py:252
  214.8 2.1 fusion.5
  216.9 0.1 slice_bitcast_fusion.3
  216.9 3.2 %collective-permute-start.10 = (bf16[16,64,128]{2,1,0:T(8,128)(2,1)S(1)}, bf16[16,64,128]{2,1,0:T(8,128)(2,1)S(1)}, u32[]{:S(2)}, u32[]{:S(2)}) collective-permute-start(bf16[16,64,128]{2,1,0:T(8,128)(2,1)S(1)} %get-tuple-element.20), channel_id=1, source_target_pairs={{0,4},{1,5},{2,6},{3,7},{4,0},{5,1},{6,2},{7,3},{8,12},{9,13},{10,... | collective-permute-start | bytes 786440 | tf_op jit(solution)/shard_map/ppermute | solution.py:249
  220.1 1.0 collective-permute-start.8
  221.2 1.0 collective-permute-start.9
  222.1 5.5 %collective-permute-done.10 = bf16[16,64,128]{2,1,0:T(8,128)(2,1)S(1)} collective-permute-done((bf16[16,64,128]{2,1,0:T(8,128)(2,1)S(1)}, bf16[16,64,128]{2,1,0:T(8,128)(2,1)S(1)}, u32[]{:S(2)}, u32[]{:S(2)}) %collective-permute-start.10) | collective-permute-done | bytes 262176 | tf_op jit(solution)/shard_map/ppermute | solution.py:249
  227.7 5.0 %collective-permute-done.8 = bf16[16,64,128]{2,1,0:T(8,128)(2,1)S(1)} collective-permute-done((bf16[16,64,128]{2,1,0:T(8,128)(2,1)S(1)}, bf16[16,64,128]{2,1,0:T(8,128)(2,1)S(1)}, u32[]{:S(2)}, u32[]{:S(2)}) %collective-permute-start.8) | collective-permute-done | bytes 262176 | tf_op jit(solution)/shard_map/ppermute | solution.py:249
  232.7 0.0 collective-permute-done.9
  232.7 0.9 copy_bitcast_fusion
  (9 shorter events, 0.0 us)
Async XLA Ops:
  6.5 93.3 %all-gather.5.cloned.1.call-start = ((), (), s32[]{:S(2)}) async-start(), calls=%async_computation.1 | async-start | bytes 8355840 | tf_op jit(solution)/shard_map/all_gather | solution.py:263
  8.0 66.2 %copy-start.1 = (s32[16,16]{1,0:T(8,128)S(1)}, s32[16,16]{1,0:T(8,128)}, u32[]{:S(2)}) copy-start(s32[16,16]{1,0:T(8,128)} %param.8) | copy-start | bytes 3076
  8.0 66.9 %copy-start.3 = (s32[128,3,1]{0,2,1:T(1,128)S(1)}, s32[128,3,1]{0,2,1:T(1,128)}, u32[]{:S(2)}) copy-start(s32[128,3,1]{0,2,1:T(1,128)} %param.9) | copy-start | bytes 4612
  12.0 153.5 %all-gather.3.cloned.1.call-start = ((), (), s32[]{:S(2)}) async-start(), calls=%async_computation | async-start | bytes 11141120 | tf_op jit(solution)/shard_map/all_gather | solution.py:264
  12.7 32.2 %collective-permute-start = (bf16[2560,256]{1,0:T(8,128)(2,1)}, bf16[2560,256]{1,0:T(8,128)(2,1)S(1)}, u32[]{:S(2)}, u32[]{:S(2)}) collective-permute-start(bf16[2560,256]{1,0:T(8,128)(2,1)} %get-tuple-element.11.refs_0_), channel_id=1, source_target_pairs={{0,2},{1,3},{2,4},{3,5},{4,6},{5,7},{6,0},{7,1},{8,10},{9,11},{10,... | collective-permute-start | bytes 3932168 | tf_op jit(solution)/shard_map/ppermute | solution.py:249
  14.5 58.0 %collective-permute-start.1 = (bf16[2560,256]{1,0:T(8,128)(2,1)}, bf16[2560,256]{1,0:T(8,128)(2,1)S(1)}, u32[]{:S(2)}, u32[]{:S(2)}) collective-permute-start(bf16[2560,256]{1,0:T(8,128)(2,1)} %get-tuple-element.11.refs_0_), channel_id=1, source_target_pairs={{0,6},{1,7},{2,0},{3,1},{4,2},{5,3},{6,4},{7,5},{8,14},{9,15},{10,... | collective-permute-start | bytes 3932168 | tf_op jit(solution)/shard_map/ppermute | solution.py:249
  16.0 58.2 %collective-permute-start.2 = (bf16[2560,256]{1,0:T(8,128)(2,1)}, bf16[2560,256]{1,0:T(8,128)(2,1)}, u32[]{:S(2)}, u32[]{:S(2)}) collective-permute-start(bf16[2560,256]{1,0:T(8,128)(2,1)} %get-tuple-element.11.refs_0_), channel_id=1, source_target_pairs={{0,4},{1,5},{2,6},{3,7},{4,0},{5,1},{6,2},{7,3},{8,12},{9,13},{10,... | collective-permute-start | bytes 3932168 | tf_op jit(solution)/shard_map/ppermute | solution.py:249
  18.1 59.0 %collective-permute-start.3 = (bf16[2560,256]{1,0:T(8,128)(2,1)}, bf16[2560,256]{1,0:T(8,128)(2,1)}, u32[]{:S(2)}, u32[]{:S(2)}) collective-permute-start(bf16[2560,256]{1,0:T(8,128)(2,1)} %get-tuple-element.11.refs_0_), channel_id=1, source_target_pairs={{0,1},{1,0},{2,3},{3,2},{4,5},{5,4},{6,7},{7,6},{8,9},{9,8},{10,11... | collective-permute-start | bytes 3932168 | tf_op jit(solution)/shard_map/ppermute | solution.py:252
  44.9 32.8 %copy-start.4 = (bf16[2560,256]{1,0:T(8,128)(2,1)}, bf16[2560,256]{1,0:T(8,128)(2,1)S(1)}, u32[]{:S(2)}) copy-start(bf16[2560,256]{1,0:T(8,128)(2,1)S(1)} %collective-permute-done.refs_1_) | copy-start | bytes 3932164
  44.9 32.2 %collective-permute-start.4 = (bf16[2560,256]{1,0:T(8,128)(2,1)S(1)}, bf16[2560,256]{1,0:T(8,128)(2,1)}, u32[]{:S(2)}, u32[]{:S(2)}) collective-permute-start(bf16[2560,256]{1,0:T(8,128)(2,1)S(1)} %collective-permute-done.refs_1_), channel_id=1, source_target_pairs={{0,1},{1,0},{2,3},{3,2},{4,5},{5,4},{6,7},{7,6},{8,9},{9,8},{10,11... | collective-permute-start | bytes 3932168 | tf_op jit(solution)/shard_map/ppermute | solution.py:252
  72.5 5.2 %copy-start.5 = (bf16[2560,256]{1,0:T(8,128)(2,1)}, bf16[2560,256]{1,0:T(8,128)(2,1)S(1)}, u32[]{:S(2)}) copy-start(bf16[2560,256]{1,0:T(8,128)(2,1)S(1)} %collective-permute-done.1.refs_2_) | copy-start | bytes 3932164
  72.5 4.7 %collective-permute-start.5 = (bf16[2560,256]{1,0:T(8,128)(2,1)S(1)}, bf16[2560,256]{1,0:T(8,128)(2,1)}, u32[]{:S(2)}, u32[]{:S(2)}) collective-permute-start(bf16[2560,256]{1,0:T(8,128)(2,1)S(1)} %collective-permute-done.1.refs_2_), channel_id=1, source_target_pairs={{0,1},{1,0},{2,3},{3,2},{4,5},{5,4},{6,7},{7,6},{8,9},{9,8},{10,11... | collective-permute-start | bytes 3932168 | tf_op jit(solution)/shard_map/ppermute | solution.py:252
  74.3 3.4 %collective-permute-start.6 = (bf16[2560,256]{1,0:T(8,128)(2,1)}, bf16[2560,256]{1,0:T(8,128)(2,1)}, u32[]{:S(2)}, u32[]{:S(2)}) collective-permute-start(bf16[2560,256]{1,0:T(8,128)(2,1)} %collective-permute-done.2.refs_3_), channel_id=1, source_target_pairs={{0,1},{1,0},{2,3},{3,2},{4,5},{5,4},{6,7},{7,6},{8,9},{9,8},{10,11... | collective-permute-start | bytes 3932168 | tf_op jit(solution)/shard_map/ppermute | solution.py:252
  75.9 24.0 %copy-start.2 = (s32[8]{0:T(128)}, s32[8]{0:T(128)S(1)}, u32[]{:S(2)}) copy-start(s32[8]{0:T(128)S(1)} %stack.35.slots) | copy-start | bytes 100
  212.0 20.6 %copy-start = (f32[16,64,128]{2,1,0:T(8,128)S(1)}, f32[16,64,128]{2,1,0:T(8,128)}, u32[]{:S(2)}) copy-start(f32[16,64,128]{2,1,0:T(8,128)} %get-tuple-element.12) | copy-start | bytes 1572868
  212.0 2.7 %collective-permute-start.7 = (bf16[4,16,64,128]{3,2,1,0:T(8,128)(2,1)S(1)}, bf16[4,16,64,128]{3,2,1,0:T(8,128)(2,1)S(1)}, u32[]{:S(2)}, u32[]{:S(2)}) collective-permute-start(bf16[4,16,64,128]{3,2,1,0:T(8,128)(2,1)S(1)} %slice.59), channel_id=1, source_target_pairs={{0,1},{1,0},{2,3},{3,2},{4,5},{5,4},{6,7},{7,6},{8,9},{9,8},{10,11... | collective-permute-start | bytes 3145736 | tf_op jit(solution)/shard_map/ppermute | solution.py:252
  216.9 10.8 %collective-permute-start.10 = (bf16[16,64,128]{2,1,0:T(8,128)(2,1)S(1)}, bf16[16,64,128]{2,1,0:T(8,128)(2,1)S(1)}, u32[]{:S(2)}, u32[]{:S(2)}) collective-permute-start(bf16[16,64,128]{2,1,0:T(8,128)(2,1)S(1)} %get-tuple-element.20), channel_id=1, source_target_pairs={{0,4},{1,5},{2,6},{3,7},{4,0},{5,1},{6,2},{7,3},{8,12},{9,13},{10,... | collective-permute-start | bytes 786440 | tf_op jit(solution)/shard_map/ppermute | solution.py:249
  220.1 12.5 %collective-permute-start.8 = (bf16[16,64,128]{2,1,0:T(8,128)(2,1)S(1)}, bf16[16,64,128]{2,1,0:T(8,128)(2,1)S(1)}, u32[]{:S(2)}, u32[]{:S(2)}) collective-permute-start(bf16[16,64,128]{2,1,0:T(8,128)(2,1)S(1)} %get-tuple-element.19), channel_id=1, source_target_pairs={{0,6},{1,7},{2,0},{3,1},{4,2},{5,3},{6,4},{7,5},{8,14},{9,15},{10,... | collective-permute-start | bytes 786440 | tf_op jit(solution)/shard_map/ppermute | solution.py:249
  221.2 11.5 %collective-permute-start.9 = (bf16[16,64,128]{2,1,0:T(8,128)(2,1)S(1)}, bf16[16,64,128]{2,1,0:T(8,128)(2,1)S(1)}, u32[]{:S(2)}, u32[]{:S(2)}) collective-permute-start(bf16[16,64,128]{2,1,0:T(8,128)(2,1)S(1)} %get-tuple-element.21), channel_id=1, source_target_pairs={{0,2},{1,3},{2,4},{3,5},{4,6},{5,7},{6,0},{7,1},{8,10},{9,11},{10,... | collective-permute-start | bytes 786440 | tf_op jit(solution)/shard_map/ppermute | solution.py:249
Sparse Core Ops, SparseCore 0:
  12.1 71.1 all-gather.4
  85.4 79.9 all-gather.2

commit v2 on v1

--- a/solution.py
+++ b/solution.py
@@ -14,17 +14,35 @@
 PTS = BLK_DEV * BLK
 PACK = PTS + BLK_DEV * 32
 NODE = RANK + WCOL
+HALF = 3 * NODE // 2
 LOG2E = 1.4426950408889634
 DOT_SCALE = 4.0 * LOG2E
 NORM_SCALE = 2.0 * LOG2E
 DEAD = 1e30
-STEP = 4
 F32 = jnp.float32
 BF16 = jnp.bfloat16
 NT = (((1,), (1,)), ((), ()))
 
 
-def prep_body(pts, wts, ewts, idx, y_out, l0_out, l12_out):
+def prep_body(pts, wts, ewts, idx, y_out, l0_out, half_a, half_b):
+    def node(r, first, size):
+        iota = lax.broadcasted_iota(jnp.int32, (RANK, size), 1)
+        pick = jnp.where(iota == idx[:, r : r + 1] - first, 1.0, 0.0).astype(BF16)
+        rows = lax.dot_general(pick, pts[first : first + size, :], (((1,), (0,)), ((), ())), preferred_element_type=F32)
+        return rows.astype(BF16)
+
+    half_a[0:RANK, :] = node(4, 0, 1024)
+    half_a[RANK:NODE, :] = ewts[4]
+    rows = node(5, 1024, 1024)
+    cut = HALF - NODE
+    half_a[NODE:HALF, :] = rows[0:cut]
+    half_b[0 : RANK - cut, :] = rows[cut:RANK]
+    half_b[RANK - cut : NODE - cut, :] = ewts[5]
+    half_b[NODE - cut : HALF - WCOL, :] = node(6, 0, 2048)
+    half_b[HALF - WCOL : HALF, :] = ewts[6]
+    for r in range(4):
+        l0_out[r * NODE : r * NODE + RANK, :] = node(r, r * 512, 512)
+        l0_out[r * NODE + RANK : (r + 1) * NODE, :] = ewts[r]
     y_out[0:PTS, :] = pts[...]
     for b in range(BLK_DEV):
         w = wts[:, b * BLK : (b + 1) * BLK]
@@ -32,19 +50,6 @@
         y_out[row : row + 32, 0:BLK] = w[0:32]
         y_out[row : row + 32, BLK:E] = w[32:64]
 
-    def node(r, first, size, out, slot):
-        iota = lax.broadcasted_iota(jnp.int32, (RANK, size), 1)
-        pick = jnp.where(iota == idx[:, r : r + 1] - first, 1.0, 0.0).astype(BF16)
-        rows = lax.dot_general(pick, pts[first : first + size, :], (((1,), (0,)), ((), ())), preferred_element_type=F32)
-        out[slot * NODE : slot * NODE + RANK, :] = rows.astype(BF16)
-        out[slot * NODE + RANK : (slot + 1) * NODE, :] = ewts[r]
-
-    node(4, 0, 1024, l12_out, 0)
-    node(5, 1024, 1024, l12_out, 1)
-    node(6, 0, 2048, l12_out, 2)
-    for r in range(4):
-        node(r, r * 512, 512, l0_out, r)
-
 
 def prep(points, weights_t, equiv_t, skel_t):
     return pl.pallas_call(
@@ -52,7 +57,8 @@
         out_shape=(
             jax.ShapeDtypeStruct((PACK, E), BF16),
             jax.ShapeDtypeStruct((4 * NODE, E), BF16),
-            jax.ShapeDtypeStruct((3 * NODE, E), BF16),
+            jax.ShapeDtypeStruct((HALF, E), BF16),
+            jax.ShapeDtypeStruct((HALF, E), BF16),
         ),
         cost_estimate=pl.CostEstimate(flops=10**9, bytes_accessed=8 * 10**6, transcendentals=0),
         name="prep",
@@ -156,84 +162,109 @@
     )(inv, near_list, *pieces)
 
 
-def far_call(name, slots, far, x_all, norms, panel, places, acc):
+def far_call(name, slots, owners, far, x_all, norms, panels, layout, nodes, places, group):
     levels = len(places)
-    panel_nodes = panel.shape[0] // NODE
-    steps = 8 * BLK_DEV // STEP
-    per_slot = BLK_DEV // STEP
-
-    def body(slots, far, *refs):
-        if acc is None:
-            x_ref, norm_ref, panel_hbm, out_ref, pan, node_norms, sem = refs
-        else:
-            x_ref, norm_ref, panel_hbm, acc_ref, out_ref, pan, node_norms, sem = refs
-        step = pl.program_id(0)
-
-        @pl.when(step == 0)
-        def _():
-            copy = pltpu.make_async_copy(panel_hbm, pan, sem)
+    count = len(panels)
+
+    def body(slots, owners, far, x_hbm, norm_ref, *refs):
+        sources = refs[:count]
+        out_hbm, xs, pan, node_norms, out_v, s0, s1, psem, xsem, osem = refs[count:]
+        panel_copies = [
+            pltpu.make_async_copy(sources[p].at[pl.ds(a, r), :], pan.at[pl.ds(place(owners), r), :], psem.at[i])
+            for i, (p, a, r, place) in enumerate(layout)
+        ]
+        x_copies = [
+            pltpu.make_async_copy(x_hbm.at[k], xs.at[pl.ds(k * PTS, PTS), :], xsem.at[k]) for k in range(8)
+        ]
+        out_copies = [pltpu.make_async_copy(out_v.at[k], out_hbm.at[k], osem.at[k]) for k in range(8)]
+        for copy in panel_copies + x_copies:
             copy.start()
+        for copy in panel_copies:
             copy.wait()
 
-            def norms_of(q, carry):
-                for u in range(4):
-                    n = q * 4 + u
-                    x = pan[pl.ds(pl.multiple_of(n * NODE, NODE), RANK), :]
-                    node_norms[pl.ds(n, 1), :] = row_norms(x)
+        def norms_of(q, carry):
+            for u in range(4):
+                n = q * 4 + u
+                x = pan[pl.ds(pl.multiple_of(n * NODE, NODE), RANK), :]
+                node_norms[pl.ds(n, 1), :] = row_norms(x)
+            return carry
+
+        lax.fori_loop(0, nodes // 4, norms_of, 0)
+
+        def entry(b, level):
+            v = far[(slots[b // BLK_DEV] * BLK_DEV + b % BLK_DEV) * levels + level]
+            n = places[level](jnp.maximum(v, 0))
+            return v, n, pl.multiple_of(n * NODE, NODE)
+
+        def dots(b0, s_ref):
+            for u in range(group):
+                x = xs[pl.ds(pl.multiple_of((b0 + u) * BLK, BLK), BLK), :]
+                col = column_of(norm_ref[pl.ds(b0 + u, 1), :])
+                for level in range(levels):
+                    _, _, row = entry(b0 + u, level)
+                    dot = lax.dot_general(x, pan[pl.ds(row, RANK), :], NT, preferred_element_type=F32)
+                    s_ref[u * levels + level] = dot * DOT_SCALE - col
+
+        def finish(b0, s_ref):
+            for u in range(group):
+                b = b0 + u
+                total = None
+                for level in range(levels):
+                    v, n, row = entry(b, level)
+                    bias = jnp.where(v >= 0, 0.0, DEAD).astype(F32)
+                    src_row = node_norms[pl.ds(n, 1), :] + bias
+                    k = jnp.exp2(s_ref[u * levels + level] - src_row).astype(BF16)
+                    wt = pan[pl.ds(row + RANK, WCOL), :]
+                    part = lax.dot_general(wt, k, NT, preferred_element_type=F32)
+                    total = part if total is None else total + part
+                out_v[b // BLK_DEV, b % BLK_DEV] = total
+
+        last = 8 * BLK_DEV - group
+        x_copies[0].wait()
+        dots(0, s0)
+        for k in range(8):
+            if k < 7:
+                x_copies[k + 1].wait()
+
+            def pair(j, carry, k=k):
+                b = k * BLK_DEV + j * 2 * group
+                dots(b + group, s1)
+                finish(b, s0)
+                dots(jnp.minimum(b + 2 * group, last), s0)
+                finish(b + group, s1)
                 return carry
 
-            lax.fori_loop(0, panel_nodes // 4, norms_of, 0)
-
-        k = step // per_slot
-        first = (step % per_slot) * STEP
-        for u in range(STEP):
-            x = x_ref[0, u * BLK : (u + 1) * BLK, :]
-            col = column_of(norm_ref[pl.ds(step * STEP + u, 1), :])
-            total = None if acc is None else acc_ref[0, u]
-            for level in range(levels):
-                v = far[(slots[k] * BLK_DEV + first + u) * levels + level]
-                n = places[level](jnp.maximum(v, 0))
-                row = pl.multiple_of(n * NODE, NODE)
-                bias = jnp.where(v >= 0, 0.0, DEAD).astype(F32)
-                part = tile(
-                    x,
-                    col,
-                    pan[pl.ds(row, RANK), :],
-                    node_norms[pl.ds(n, 1), :] + bias,
-                    pan[pl.ds(row + RANK, WCOL), :],
-                )
-                total = part if total is None else total + part
-            out_ref[0, u] = total
-
-    blocked = pl.BlockSpec((1, STEP, WCOL, BLK), lambda s, *_: (s // per_slot, s % per_slot, 0, 0))
-    in_specs = [
-        pl.BlockSpec((1, STEP * BLK, E), lambda s, *_: (s // per_slot, s % per_slot, 0)),
-        pl.BlockSpec((8 * BLK_DEV, BLK), lambda s, *_: (0, 0)),
-        pl.BlockSpec(memory_space=pl.ANY),
-    ]
-    operands = [x_all, norms, panel]
-    if acc is not None:
-        in_specs.append(blocked)
-        operands.append(acc)
+            lax.fori_loop(0, BLK_DEV // (2 * group), pair, 0)
+            out_copies[k].start()
+        for copy in out_copies:
+            copy.wait()
+
+    anys = pl.BlockSpec(memory_space=pl.ANY)
     return pl.pallas_call(
         body,
         grid_spec=pltpu.PrefetchScalarGridSpec(
-            num_scalar_prefetch=2,
-            grid=(steps,),
-            in_specs=in_specs,
-            out_specs=blocked,
+            num_scalar_prefetch=3,
+            grid=(),
+            in_specs=[anys, pl.BlockSpec(memory_space=pltpu.VMEM)] + [anys] * count,
+            out_specs=anys,
             scratch_shapes=[
-                pltpu.VMEM(panel.shape, BF16),
-                pltpu.VMEM((panel_nodes, RANK), F32),
-                pltpu.SemaphoreType.DMA,
+                pltpu.VMEM((8 * PTS, E), BF16),
+                pltpu.VMEM((nodes * NODE, E), BF16),
+                pltpu.VMEM((nodes, RANK), F32),
+                pltpu.VMEM((8, BLK_DEV, WCOL, BLK), F32),
+                pltpu.VMEM((group * levels, BLK, RANK), F32),
+                pltpu.VMEM((group * levels, BLK, RANK), F32),
+                pltpu.SemaphoreType.DMA((len(layout),)),
+                pltpu.SemaphoreType.DMA((8,)),
+                pltpu.SemaphoreType.DMA((8,)),
             ],
         ),
         out_shape=jax.ShapeDtypeStruct((8, BLK_DEV, WCOL, BLK), F32),
         cost_estimate=pl.CostEstimate(
-            flops=levels * 5 * 10**9, bytes_accessed=25 * 10**6, transcendentals=levels * 4 * 10**6
+            flops=levels * 8 * 10**9, bytes_accessed=25 * 10**6, transcendentals=levels * 4 * 10**6
         ),
         name=name,
-    )(slots, far, *operands)
+    )(slots, owners, far, x_all, norms, *panels)
 
 
 def shards(points, weights, near_list, far_list, skel_index, equiv_weights):
@@ -257,17 +288,56 @@
     inv = jnp.sum(jnp.where(slots[:, None] == jnp.arange(8)[None, :], jnp.arange(8)[:, None], 0), axis=0)
     slots, inv = slots.astype(jnp.int32), inv.astype(jnp.int32)
 
-    pack, l0, l12 = prep(points, weights.T, jnp.swapaxes(equiv_weights, 1, 2), skel_index.T)
+    def along_z(d):
+        return [(t, ((t // 4 + d) % 4) * 4 + t % 4) for t in range(16)]
+
+    def along_x(d):
+        return [(t, (t // 4) * 4 + (t % 4 + d) % 4) for t in range(16)]
+
+    def move(v, pairs):
+        return lax.ppermute(v, "tgt", pairs)
+
+    def first_axis(v, along):
+        return jnp.concatenate([v, move(v, along(1)), move(v, along(-1)), move(v, along(2))], axis=0)
+
+    def second_axis(v, along):
+        n = v.shape[0] // 2
+        up, down = move(v, along(1)), move(v, along(-1))
+        return [v, up, down, move(up[:n], along(1)), move(down[n:], along(-1))]
+
+    tgt_index = lax.axis_index("tgt")
+    offsets = jnp.array([0, 3, 1, 2], jnp.int32)
+    zs, xs = (tgt_index // 4 + offsets) % 4, (tgt_index % 4 + offsets) % 4
+    owners = (zs[:, None] * 4 + xs[None, :]).reshape(-1).astype(jnp.int32)
+
+    pack, l0, half_a, half_b = prep(points, weights.T, jnp.swapaxes(equiv_weights, 1, 2), skel_index.T)
+    panel0 = lax.all_gather(l0, "tgt", axis=0, tiled=True)
+    panels12 = second_axis(first_axis(half_a, along_z), along_x) + second_axis(first_axis(half_b, along_x), along_z)
     mine = [pack, shift(pack, 1), shift(pack, -1), shift(pack, 2)]
     pieces = mine + [swap(v) for v in mine]
-    panel12 = lax.all_gather(l12, "tgt", axis=0, tiled=True)
-    panel0 = lax.all_gather(l0, "tgt", axis=0, tiled=True)
+
+    layout12 = []
+    for half in range(2):
+        for far_step in range(4):
+            for near_step in range(4):
+                panel, row = (far_step, near_step) if far_step < 3 else (3 + near_step // 2, near_step % 2)
+                owner = near_step * 4 + far_step if half == 0 else far_step * 4 + near_step
+                layout12.append(
+                    (
+                        half * 5 + panel,
+                        row * HALF,
+                        HALF,
+                        lambda o, owner=owner, half=half: pl.multiple_of(o[owner] * (2 * HALF) + half * HALF, 32),
+                    )
+                )
 
     x_all, norms, near_sum = near_call(inv, near_list.reshape(-1), pieces)
     far = far_list[:, :, 0]
     places12 = (lambda v: (v // 2) * 3 + v % 2, lambda v: v * 3 + 2)
-    far12 = far_call("far12", slots, far[:, 1:].reshape(-1), x_all, norms, panel12, places12, None)
-    total = far_call("far0", slots, far[:, 0].reshape(-1), x_all, norms, panel0, (lambda v: v,), far12)
+    far12 = far_call("far12", slots, owners, far[:, 1:].reshape(-1), x_all, norms, panels12, layout12, 48, places12, 4)
+    layout0 = [(0, i * 4 * NODE, 4 * NODE, lambda o, i=i: i * 4 * NODE) for i in range(16)]
+    far0 = far_call("far0", slots, owners, far[:, 0].reshape(-1), x_all, norms, [panel0], layout0, 64, (lambda v: v,), 4)
+    total = far12 + far0
 
     chip = total[0:4] + swap(total[4:8].astype(BF16)).astype(F32)
     got = [

time: 242 us -> 271 us (1.12)
  Pallas kernels: 119 us -> 79.1 us
  waiting for transfers between devices: 88.1 us -> 121 us
  starting transfers between devices: 10.8 us -> 37.3 us
  local copies, waits for them, and re-layouts: 5.5 us -> 12.7 us
  other arithmetic: 3.65 us -> 6.45 us
    ppermute x0 -> x14, waiting for transfers between devices: none -> 106 us  [move(): return lax.ppermute(v, 'tgt', pairs)]
    ppermute x6, waiting for transfers between devices: 66.6 us -> 12.6 us  [shift(): return lax.ppermute(v, 'src', along_y(d))]
    pallas_call x2, Pallas kernels: 92.8 us -> 53 us  [far_call(): pl.pallas_call(body, grid_spec=pltpu.PrefetchScalarGridSpec(num_scalar_pr...]
    ppermute x0 -> x14, starting transfers between devices: none -> 24.8 us  [move(): return lax.ppermute(v, 'tgt', pairs)]
    all_gather x1, waiting for transfers between devices: 17.6 us -> 0.02 us  [shards(): panel0 = lax.all_gather(l0, 'tgt', axis=0, tiled=True)]
    add x0 -> x2, other arithmetic: none -> 4.47 us  [the longest x1 4.4 us: shards(): total = far12 + far0]
    unnamed x14 -> x30, local copies, waits for them, and re-layouts: 1.52 us -> 5.75 us
    slice x0 -> x4, local copies, waits for them, and re-layouts: none -> 3.22 us  [second_axis(): return [v, up, down, move(up[:n], along(1)), move(down[n:], along(-1))]]
  transfers between devices with their start and end apart: 13 -> 26, of which waited for: 8 -> 10; matrix products, arithmetic and copies ran while one was open for 1% -> 4% of each run, Pallas kernels for 29% -> 19%
where the time goes in v2:
time: 271 us; the launch traced here: 270 us
  waiting for transfers between devices  121 us (45%)
  Pallas kernels  79.1 us (29%)
  starting transfers between devices  37.3 us (14%)
  between operations  13.6 us (5%)
  local copies, waits for them, and re-layouts  12.7 us (5%)
  other arithmetic  6.45 us (2%)
    ppermute x14, waiting for transfers between devices, move(): return lax.ppermute(v, 'tgt', pairs)  106 us
    pallas_call x2, Pallas kernels, far_call(): pl.pallas_call(body, grid_spec=pltpu.PrefetchScalarGridSpec(num_scalar_pr...  53 us
    ppermute x14, starting transfers between devices, move(): return lax.ppermute(v, 'tgt', pairs)  24.8 us
    pallas_call x1, Pallas kernels, near_call(): pl.pallas_call(near_body, grid_spec=pltpu.PrefetchScalarGridSpec(num_scal...  22.2 us
    ppermute x6, waiting for transfers between devices, shift(): return lax.ppermute(v, 'src', along_y(d))  12.6 us
    ppermute x6, starting transfers between devices, shift(): return lax.ppermute(v, 'src', along_y(d))  11.3 us
    unnamed x30, local copies, waits for them, and re-layouts  5.75 us
  transfers between devices with their start and end apart: 26, of which 10 were waited for; matrix products, arithmetic and copies ran while one was open for 4% of the time, Pallas kernels for 19%

profile of v2, /device:TPU:0, one launch (start us, length us, event | category | flops | bytes accessed | tf_op | source)
XLA Modules:
  0.0 270.3 jit_solution(9198469457872956698)
XLA Ops:
  6.5 1.5 copy.12
  8.0 3.9 %prep.1 = (bf16[2560,256]{1,0:T(8,128)(2,1)}, bf16[1280,256]{1,0:T(8,128)(2,1)}, bf16[480,256]{1,0:T(8,128)(2,1)}, bf16[480,256]{1,0:T(8,128)(2,1)}) custom-call(bf16[2048,256]{1,0:T(8,128)(2,1)} %pts.1, bf16[64,2048]{1,0:T(8,128)(2,1)} %bitcast.44, bf16[7,64,256]{2,1,0:T(8,128)(2,1)} %bitcast.45, s32[256,7]{1,0:T(8,128)} %bitcast.41), custom_call_target="tpu_custom_call" | custom-call | flops 1000000000 | bytes 8000000 | tf_op jit(solution)/shard_map/prep/pallas_call | solution.py:55
  12.0 2.1 collective-permute-start.7
  14.1 2.2 collective-permute-start.8
  16.3 1.8 collective-permute-start.9
  18.1 1.0 constant_dynamic-update-slice_fusion.3
  19.1 3.3 %collective-permute-done.7 = bf16[480,256]{1,0:T(8,128)(2,1)S(1)} collective-permute-done((bf16[480,256]{1,0:T(8,128)(2,1)}, bf16[480,256]{1,0:T(8,128)(2,1)S(1)}, u32[]{:S(2)}, u32[]{:S(2)}) %collective-permute-start.7) | collective-permute-done | bytes 245792 | tf_op jit(solution)/shard_map/ppermute | solution.py:298
  22.4 6.1 %collective-permute-done.8 = bf16[480,256]{1,0:T(8,128)(2,1)S(1)} collective-permute-done((bf16[480,256]{1,0:T(8,128)(2,1)}, bf16[480,256]{1,0:T(8,128)(2,1)S(1)}, u32[]{:S(2)}, u32[]{:S(2)}) %collective-permute-start.8) | collective-permute-done | bytes 245792 | tf_op jit(solution)/shard_map/ppermute | solution.py:298
  28.8 1.6 collective-permute-start.10
  30.4 1.5 collective-permute-start.14
  31.9 1.7 collective-permute-start.15
  33.6 1.6 collective-permute-start
  35.2 1.7 collective-permute-start.1
  36.9 35.3 %collective-permute-done.14 = bf16[480,256]{1,0:T(8,128)(2,1)S(1)} collective-permute-done((bf16[480,256]{1,0:T(8,128)(2,1)S(1)}, bf16[480,256]{1,0:T(8,128)(2,1)S(1)}, u32[]{:S(2)}, u32[]{:S(2)}) %collective-permute-start.14) | collective-permute-done | bytes 245792 | tf_op jit(solution)/shard_map/ppermute | solution.py:298
  72.2 3.0 %collective-permute-start.2 = (bf16[2560,256]{1,0:T(8,128)(2,1)}, bf16[2560,256]{1,0:T(8,128)(2,1)}, u32[]{:S(2)}, u32[]{:S(2)}) collective-permute-start(bf16[2560,256]{1,0:T(8,128)(2,1)} %get-tuple-element.12.refs_0_), channel_id=1, source_target_pairs={{0,4},{1,5},{2,6},{3,7},{4,0},{5,1},{6,2},{7,3},{8,12},{9,13},{10,... | collective-permute-start | bytes 3932168 | tf_op jit(solution)/shard_map/ppermute | solution.py:280
  75.2 1.3 collective-permute-start.16
  76.5 0.7 constant_dynamic-update-slice_fusion.7
  77.2 12.5 %collective-permute-done.16 = bf16[480,256]{1,0:T(8,128)(2,1)S(1)} collective-permute-done((bf16[480,256]{1,0:T(8,128)(2,1)S(1)}, bf16[480,256]{1,0:T(8,128)(2,1)S(1)}, u32[]{:S(2)}, u32[]{:S(2)}) %collective-permute-start.16) | collective-permute-done | bytes 245792 | tf_op jit(solution)/shard_map/ppermute | solution.py:298
  89.8 0.8 collective-permute-start.11
  90.6 0.7 constant_dynamic-update-slice_fusion.6
  91.3 0.7 constant_dynamic-update-slice_fusion.5
  92.0 0.7 constant_dynamic-update-slice_fusion.4.refs_5_
  92.7 1.6 collective-permute-start.17
  94.3 32.4 %collective-permute-done.11.refs_2_ = bf16[1920,256]{1,0:T(8,128)(2,1)} collective-permute-done((bf16[1920,256]{1,0:T(8,128)(2,1)S(1)}, bf16[1920,256]{1,0:T(8,128)(2,1)}, u32[]{:S(2)}, u32[]{:S(2)}) %collective-permute-start.11) | collective-permute-done | bytes 983072 | tf_op jit(solution)/shard_map/ppermute | solution.py:298
  127.7 2.9 %collective-permute-start.18 = (bf16[1920,256]{1,0:T(8,128)(2,1)}, bf16[1920,256]{1,0:T(8,128)(2,1)}, u32[]{:S(2)}, u32[]{:S(2)}) collective-permute-start(bf16[1920,256]{1,0:T(8,128)(2,1)} %constant_dynamic-update-slice_fusion.4.refs_5_), channel_id=1, source_target_pairs={{0,96},{8,104},{16,112},{24,120},{32,0},{40,8},{48,16},{56,24},{64... | collective-permute-start | bytes 2949128 | tf_op jit(solution)/shard_map/ppermute | solution.py:298
  130.6 0.7 reshape.20.near
  131.4 0.6 add.137.owners
  132.1 0.7 reshape.21.far
  133.0 0.6 select_reduce_fusion.inv
  134.1 1.1 slice.53
  135.2 1.1 slice.54
  136.2 16.0 %collective-permute-done.18.refs_7_ = bf16[1920,256]{1,0:T(8,128)(2,1)} collective-permute-done((bf16[1920,256]{1,0:T(8,128)(2,1)}, bf16[1920,256]{1,0:T(8,128)(2,1)}, u32[]{:S(2)}, u32[]{:S(2)}) %collective-permute-start.18) | collective-permute-done | bytes 983072 | tf_op jit(solution)/shard_map/ppermute | solution.py:298
  152.2 1.5 collective-permute-start.12
  153.7 1.1 slice.55
  154.8 1.8 collective-permute-start.13
  156.6 1.1 collective-permute-start.19
  157.7 2.9 %collective-permute-start.20 = (bf16[960,256]{1,0:T(8,128)(2,1)S(1)}, bf16[960,256]{1,0:T(8,128)(2,1)}, u32[]{:S(2)}, u32[]{:S(2)}) collective-permute-start(bf16[960,256]{1,0:T(8,128)(2,1)S(1)} %slice.55), channel_id=1, source_target_pairs={{0,96},{8,104},{16,112},{24,120},{32,0},{40,8},{48,16},{56,24},{64... | collective-permute-start | bytes 1474568 | tf_op jit(solution)/shard_map/ppermute | solution.py:298
  160.6 22.2 %near.1 = (bf16[8,2048,256]{2,1,0:T(8,128)(2,1)}, f32[128,128]{1,0:T(8,128)}, f32[16,64,128]{2,1,0:T(8,128)}) custom-call(s32[8]{0:T(128)} %select_reduce_fusion.inv, s32[256]{0:T(256)} %reshape.20.near, bf16[2560,256]{1,0:T(8,128)(2,1)} %get-tuple-element.12.refs_0_, bf16[2560,256]{1,0:T(8,128)(2,1)} %collective-permute-done.refs_1_, ...), custom_call_target="tpu_custom_call" | custom-call | flops 6000000000 | bytes 20000000 | tf_op jit(solution)/shard_map/near/pallas_call | solution.py:142
  182.8 0.7 copy-done.8
  183.9 30.1 %far12.1 = f32[8,16,64,128]{3,2,1,0:T(8,128)} custom-call(s32[8]{0:T(128)} %copy-done.7, s32[16]{0:T(128)} %add.137.owners, s32[256]{0:T(256)} %reshape.21.far, bf16[8,2048,256]{2,1,0:T(8,128)(2,1)} %get-tuple-element.14.x_hbm, f32[128,128]{1,0:T(8,128)} %get-tuple-element.15.norm_ref, bf16[1920,256]{1,0:T(8,128)(2,1)} %copy-done.3, ...), custom_call_target="tpu_custom_call" | custom-call | flops 16000000000 | bytes 25000000 | tf_op jit(solution)/shard_map/far12/pallas_call | solution.py:243
  214.0 22.9 %far0.1 = f32[8,16,64,128]{3,2,1,0:T(8,128)} custom-call(s32[8]{0:T(128)} %copy-done.7, s32[16]{0:T(128)} %add.137.owners, s32[128]{0:T(128)} %slice_bitcast_fusion.4.far, bf16[8,2048,256]{2,1,0:T(8,128)(2,1)} %get-tuple-element.14.x_hbm, f32[128,128]{1,0:T(8,128)} %get-tuple-element.15.norm_ref, bf16[20480,256]{1,0:T(8,128)(2,1)} %all-gather.2.cloned.1.call-done.refs_0_), custom_call_target="tpu_custom_call" | custom-call | flops 8000000000 | bytes 25000000 | tf_op jit(solution)/shard_map/far0/pallas_call | solution.py:243
  237.0 4.4 %add.138 = f32[8,16,64,128]{3,2,1,0:T(8,128)S(1)} add(f32[8,16,64,128]{3,2,1,0:T(8,128)} %far12.1, f32[8,16,64,128]{3,2,1,0:T(8,128)} %far0.1) | non-fusion elementwise | flops 1048576 | bytes 12582912 | tf_op jit(solution)/shard_map/add | solution.py:340
  241.7 2.6 collective-permute-done.21
  244.8 2.8 %collective-permute-start.22 = (bf16[16,64,128]{2,1,0:T(8,128)(2,1)S(1)}, bf16[16,64,128]{2,1,0:T(8,128)(2,1)S(1)}, u32[]{:S(2)}, u32[]{:S(2)}) collective-permute-start(bf16[16,64,128]{2,1,0:T(8,128)(2,1)S(1)} %get-tuple-element.21), channel_id=1, source_target_pairs={{0,6},{1,7},{2,0},{3,1},{4,2},{5,3},{6,4},{7,5},{8,14},{9,15},{10,... | collective-permute-start | bytes 786440 | tf_op jit(solution)/shard_map/ppermute | solution.py:280
  247.6 2.3 collective-permute-start.24
  249.9 9.2 %collective-permute-done.22 = bf16[16,64,128]{2,1,0:T(8,128)(2,1)S(1)} collective-permute-done((bf16[16,64,128]{2,1,0:T(8,128)(2,1)S(1)}, bf16[16,64,128]{2,1,0:T(8,128)(2,1)S(1)}, u32[]{:S(2)}, u32[]{:S(2)}) %collective-permute-start.22) | collective-permute-done | bytes 262176 | tf_op jit(solution)/shard_map/ppermute | solution.py:280
  259.1 3.4 %collective-permute-done.23 = bf16[16,64,128]{2,1,0:T(8,128)(2,1)S(1)} collective-permute-done((bf16[16,64,128]{2,1,0:T(8,128)(2,1)S(1)}, bf16[16,64,128]{2,1,0:T(8,128)(2,1)S(1)}, u32[]{:S(2)}, u32[]{:S(2)}) %collective-permute-start.23) | collective-permute-done | bytes 262176 | tf_op jit(solution)/shard_map/ppermute | solution.py:280
  262.5 0.9 copy_bitcast_fusion
  (60 shorter events, 3.4 us)
Async XLA Ops:
  6.5 207.5 %all-gather.2.cloned.1.call-start = ((), (), s32[]{:S(2)}) async-start(), calls=%async_computation | async-start | bytes 11141120 | tf_op jit(solution)/shard_map/all_gather | solution.py:314
  11.9 18.5 %copy-start.2 = (bf16[480,256]{1,0:T(8,128)(2,1)S(1)}, bf16[480,256]{1,0:T(8,128)(2,1)}, u32[]{:S(2)}) copy-start(bf16[480,256]{1,0:T(8,128)(2,1)} %get-tuple-element.17) | copy-start | bytes 737284
  11.9 118.7 %copy-start.4 = (s32[16,16]{1,0:T(8,128)S(1)}, s32[16,16]{1,0:T(8,128)}, u32[]{:S(2)}) copy-start(s32[16,16]{1,0:T(8,128)} %param.9) | copy-start | bytes 3076
  12.0 119.4 %copy-start.6 = (s32[4]{0:T(128)S(1)}, s32[4]{0:T(128)}, u32[]{:S(2)}) copy-start(s32[4]{0:T(128)} %constant.86.clone) | copy-start | bytes 52
  12.0 120.0 %copy-start.5 = (s32[128,3,1]{0,2,1:T(1,128)S(1)}, s32[128,3,1]{0,2,1:T(1,128)}, u32[]{:S(2)}) copy-start(s32[128,3,1]{0,2,1:T(1,128)} %param.10) | copy-start | bytes 4612
  12.0 10.4 %collective-permute-start.7 = (bf16[480,256]{1,0:T(8,128)(2,1)}, bf16[480,256]{1,0:T(8,128)(2,1)S(1)}, u32[]{:S(2)}, u32[]{:S(2)}) collective-permute-start(bf16[480,256]{1,0:T(8,128)(2,1)} %get-tuple-element.16), channel_id=1, source_target_pairs={{0,32},{8,40},{16,48},{24,56},{32,64},{40,72},{48,80},{56,88},{64,... | collective-permute-start | bytes 737288 | tf_op jit(solution)/shard_map/ppermute | solution.py:298
  14.1 14.4 %collective-permute-start.8 = (bf16[480,256]{1,0:T(8,128)(2,1)}, bf16[480,256]{1,0:T(8,128)(2,1)S(1)}, u32[]{:S(2)}, u32[]{:S(2)}) collective-permute-start(bf16[480,256]{1,0:T(8,128)(2,1)} %get-tuple-element.16), channel_id=1, source_target_pairs={{0,96},{8,104},{16,112},{24,120},{32,0},{40,8},{48,16},{56,24},{64... | collective-permute-start | bytes 737288 | tf_op jit(solution)/shard_map/ppermute | solution.py:298
  16.3 12.5 %collective-permute-start.9 = (bf16[480,256]{1,0:T(8,128)(2,1)}, bf16[480,256]{1,0:T(8,128)(2,1)S(1)}, u32[]{:S(2)}, u32[]{:S(2)}) collective-permute-start(bf16[480,256]{1,0:T(8,128)(2,1)} %get-tuple-element.16), channel_id=1, source_target_pairs={{0,64},{8,72},{16,80},{24,88},{32,96},{40,104},{48,112},{56,120},{... | collective-permute-start | bytes 737288 | tf_op jit(solution)/shard_map/ppermute | solution.py:298
  28.8 104.7 %copy-start.3 = (bf16[1920,256]{1,0:T(8,128)(2,1)}, bf16[1920,256]{1,0:T(8,128)(2,1)S(1)}, u32[]{:S(2)}) copy-start(bf16[1920,256]{1,0:T(8,128)(2,1)S(1)} %constant_dynamic-update-slice_fusion.refs_0_) | copy-start | bytes 2949124
  28.8 63.9 %collective-permute-start.10 = (bf16[1920,256]{1,0:T(8,128)(2,1)S(1)}, bf16[1920,256]{1,0:T(8,128)(2,1)S(1)}, u32[]{:S(2)}, u32[]{:S(2)}) collective-permute-start(bf16[1920,256]{1,0:T(8,128)(2,1)S(1)} %constant_dynamic-update-slice_fusion.refs_0_), channel_id=1, source_target_pairs={{0,8},{8,16},{16,24},{24,0},{32,40},{40,48},{48,56},{56,32},{64,72... | collective-permute-start | bytes 2949128 | tf_op jit(solution)/shard_map/ppermute | solution.py:298
  30.4 41.8 %collective-permute-start.14 = (bf16[480,256]{1,0:T(8,128)(2,1)S(1)}, bf16[480,256]{1,0:T(8,128)(2,1)S(1)}, u32[]{:S(2)}, u32[]{:S(2)}) collective-permute-start(bf16[480,256]{1,0:T(8,128)(2,1)S(1)} %copy-done.2), channel_id=1, source_target_pairs={{0,8},{8,16},{16,24},{24,0},{32,40},{40,48},{48,56},{56,32},{64,72... | collective-permute-start | bytes 737288 | tf_op jit(solution)/shard_map/ppermute | solution.py:298
  31.9 43.3 %collective-permute-start.15 = (bf16[480,256]{1,0:T(8,128)(2,1)S(1)}, bf16[480,256]{1,0:T(8,128)(2,1)S(1)}, u32[]{:S(2)}, u32[]{:S(2)}) collective-permute-start(bf16[480,256]{1,0:T(8,128)(2,1)S(1)} %copy-done.2), channel_id=1, source_target_pairs={{0,24},{8,0},{16,8},{24,16},{32,56},{40,32},{48,40},{56,48},{64,88... | collective-permute-start | bytes 737288 | tf_op jit(solution)/shard_map/ppermute | solution.py:298
  33.6 93.0 %collective-permute-start = (bf16[2560,256]{1,0:T(8,128)(2,1)}, bf16[2560,256]{1,0:T(8,128)(2,1)}, u32[]{:S(2)}, u32[]{:S(2)}) collective-permute-start(bf16[2560,256]{1,0:T(8,128)(2,1)} %get-tuple-element.12.refs_0_), channel_id=1, source_target_pairs={{0,2},{1,3},{2,4},{3,5},{4,6},{5,7},{6,0},{7,1},{8,10},{9,11},{10,... | collective-permute-start | bytes 3932168 | tf_op jit(solution)/shard_map/ppermute | solution.py:280
  35.2 92.0 %collective-permute-start.1 = (bf16[2560,256]{1,0:T(8,128)(2,1)}, bf16[2560,256]{1,0:T(8,128)(2,1)}, u32[]{:S(2)}, u32[]{:S(2)}) collective-permute-start(bf16[2560,256]{1,0:T(8,128)(2,1)} %get-tuple-element.12.refs_0_), channel_id=1, source_target_pairs={{0,6},{1,7},{2,0},{3,1},{4,2},{5,3},{6,4},{7,5},{8,14},{9,15},{10,... | collective-permute-start | bytes 3932168 | tf_op jit(solution)/shard_map/ppermute | solution.py:280
  72.2 55.1 %collective-permute-start.2 = (bf16[2560,256]{1,0:T(8,128)(2,1)}, bf16[2560,256]{1,0:T(8,128)(2,1)}, u32[]{:S(2)}, u32[]{:S(2)}) collective-permute-start(bf16[2560,256]{1,0:T(8,128)(2,1)} %get-tuple-element.12.refs_0_), channel_id=1, source_target_pairs={{0,4},{1,5},{2,6},{3,7},{4,0},{5,1},{6,2},{7,3},{8,12},{9,13},{10,... | collective-permute-start | bytes 3932168 | tf_op jit(solution)/shard_map/ppermute | solution.py:280
  75.2 14.6 %collective-permute-start.16 = (bf16[480,256]{1,0:T(8,128)(2,1)S(1)}, bf16[480,256]{1,0:T(8,128)(2,1)S(1)}, u32[]{:S(2)}, u32[]{:S(2)}) collective-permute-start(bf16[480,256]{1,0:T(8,128)(2,1)S(1)} %copy-done.2), channel_id=1, source_target_pairs={{0,16},{8,24},{16,0},{24,8},{32,48},{40,56},{48,32},{56,40},{64,80... | collective-permute-start | bytes 737288 | tf_op jit(solution)/shard_map/ppermute | solution.py:298
  89.8 36.9 %collective-permute-start.11 = (bf16[1920,256]{1,0:T(8,128)(2,1)S(1)}, bf16[1920,256]{1,0:T(8,128)(2,1)}, u32[]{:S(2)}, u32[]{:S(2)}) collective-permute-start(bf16[1920,256]{1,0:T(8,128)(2,1)S(1)} %constant_dynamic-update-slice_fusion.refs_0_), channel_id=1, source_target_pairs={{0,24},{8,0},{16,8},{24,16},{32,56},{40,32},{48,40},{56,48},{64,88... | collective-permute-start | bytes 2949128 | tf_op jit(solution)/shard_map/ppermute | solution.py:298
  92.7 62.0 %copy-start.1 = (bf16[1920,256]{1,0:T(8,128)(2,1)}, bf16[1920,256]{1,0:T(8,128)(2,1)S(1)}, u32[]{:S(2)}) copy-start(bf16[1920,256]{1,0:T(8,128)(2,1)S(1)} %collective-permute-done.10.refs_1_) | copy-start | bytes 2949124
  92.7 34.9 %collective-permute-start.17 = (bf16[1920,256]{1,0:T(8,128)(2,1)}, bf16[1920,256]{1,0:T(8,128)(2,1)}, u32[]{:S(2)}, u32[]{:S(2)}) collective-permute-start(bf16[1920,256]{1,0:T(8,128)(2,1)} %constant_dynamic-update-slice_fusion.4.refs_5_), channel_id=1, source_target_pairs={{0,32},{8,40},{16,48},{24,56},{32,64},{40,72},{48,80},{56,88},{64,... | collective-permute-start | bytes 2949128 | tf_op jit(solution)/shard_map/ppermute | solution.py:298
  126.7 28.1 %collective-permute-start.3 = (bf16[2560,256]{1,0:T(8,128)(2,1)}, bf16[2560,256]{1,0:T(8,128)(2,1)}, u32[]{:S(2)}, u32[]{:S(2)}) collective-permute-start(bf16[2560,256]{1,0:T(8,128)(2,1)} %get-tuple-element.12.refs_0_), channel_id=1, source_target_pairs={{0,1},{1,0},{2,3},{3,2},{4,5},{5,4},{6,7},{7,6},{8,9},{9,8},{10,11... | collective-permute-start | bytes 3932168 | tf_op jit(solution)/shard_map/ppermute | solution.py:283
  126.7 30.0 %collective-permute-start.4 = (bf16[2560,256]{1,0:T(8,128)(2,1)}, bf16[2560,256]{1,0:T(8,128)(2,1)}, u32[]{:S(2)}, u32[]{:S(2)}) collective-permute-start(bf16[2560,256]{1,0:T(8,128)(2,1)} %collective-permute-done.refs_1_), channel_id=1, source_target_pairs={{0,1},{1,0},{2,3},{3,2},{4,5},{5,4},{6,7},{7,6},{8,9},{9,8},{10,11... | collective-permute-start | bytes 3932168 | tf_op jit(solution)/shard_map/ppermute | solution.py:283
  127.2 30.5 %collective-permute-start.5 = (bf16[2560,256]{1,0:T(8,128)(2,1)}, bf16[2560,256]{1,0:T(8,128)(2,1)}, u32[]{:S(2)}, u32[]{:S(2)}) collective-permute-start(bf16[2560,256]{1,0:T(8,128)(2,1)} %collective-permute-done.1.refs_2_), channel_id=1, source_target_pairs={{0,1},{1,0},{2,3},{3,2},{4,5},{5,4},{6,7},{7,6},{8,9},{9,8},{10,11... | collective-permute-start | bytes 3932168 | tf_op jit(solution)/shard_map/ppermute | solution.py:283
  127.3 33.3 %collective-permute-start.6 = (bf16[2560,256]{1,0:T(8,128)(2,1)}, bf16[2560,256]{1,0:T(8,128)(2,1)}, u32[]{:S(2)}, u32[]{:S(2)}) collective-permute-start(bf16[2560,256]{1,0:T(8,128)(2,1)} %collective-permute-done.2.refs_3_), channel_id=1, source_target_pairs={{0,1},{1,0},{2,3},{3,2},{4,5},{5,4},{6,7},{7,6},{8,9},{9,8},{10,11... | collective-permute-start | bytes 3932168 | tf_op jit(solution)/shard_map/ppermute | solution.py:283
  127.7 24.5 %collective-permute-start.18 = (bf16[1920,256]{1,0:T(8,128)(2,1)}, bf16[1920,256]{1,0:T(8,128)(2,1)}, u32[]{:S(2)}, u32[]{:S(2)}) collective-permute-start(bf16[1920,256]{1,0:T(8,128)(2,1)} %constant_dynamic-update-slice_fusion.4.refs_5_), channel_id=1, source_target_pairs={{0,96},{8,104},{16,112},{24,120},{32,0},{40,8},{48,16},{56,24},{64... | collective-permute-start | bytes 2949128 | tf_op jit(solution)/shard_map/ppermute | solution.py:298
  133.0 49.8 %copy-start.7 = (s32[8]{0:T(128)}, s32[8]{0:T(128)S(1)}, u32[]{:S(2)}) copy-start(s32[8]{0:T(128)S(1)} %stack.35.slots) | copy-start | bytes 100
  152.2 30.6 %collective-permute-start.12 = (bf16[960,256]{1,0:T(8,128)(2,1)S(1)}, bf16[960,256]{1,0:T(8,128)(2,1)S(1)}, u32[]{:S(2)}, u32[]{:S(2)}) collective-permute-start(bf16[960,256]{1,0:T(8,128)(2,1)S(1)} %slice.52), channel_id=1, source_target_pairs={{0,8},{8,16},{16,24},{24,0},{32,40},{40,48},{48,56},{56,32},{64,72... | collective-permute-start | bytes 1474568 | tf_op jit(solution)/shard_map/ppermute | solution.py:298
  154.8 28.0 %collective-permute-start.13 = (bf16[960,256]{1,0:T(8,128)(2,1)S(1)}, bf16[960,256]{1,0:T(8,128)(2,1)S(1)}, u32[]{:S(2)}, u32[]{:S(2)}) collective-permute-start(bf16[960,256]{1,0:T(8,128)(2,1)S(1)} %slice.53), channel_id=1, source_target_pairs={{0,24},{8,0},{16,8},{24,16},{32,56},{40,32},{48,40},{56,48},{64,88... | collective-permute-start | bytes 1474568 | tf_op jit(solution)/shard_map/ppermute | solution.py:298
  156.6 26.2 %collective-permute-start.19 = (bf16[960,256]{1,0:T(8,128)(2,1)S(1)}, bf16[960,256]{1,0:T(8,128)(2,1)S(1)}, u32[]{:S(2)}, u32[]{:S(2)}) collective-permute-start(bf16[960,256]{1,0:T(8,128)(2,1)S(1)} %slice.54), channel_id=1, source_target_pairs={{0,32},{8,40},{16,48},{24,56},{32,64},{40,72},{48,80},{56,88},{64,... | collective-permute-start | bytes 1474568 | tf_op jit(solution)/shard_map/ppermute | solution.py:298
  157.7 25.1 %collective-permute-start.20 = (bf16[960,256]{1,0:T(8,128)(2,1)S(1)}, bf16[960,256]{1,0:T(8,128)(2,1)}, u32[]{:S(2)}, u32[]{:S(2)}) collective-permute-start(bf16[960,256]{1,0:T(8,128)(2,1)S(1)} %slice.55), channel_id=1, source_target_pairs={{0,96},{8,104},{16,112},{24,120},{32,0},{40,8},{48,16},{56,24},{64... | collective-permute-start | bytes 1474568 | tf_op jit(solution)/shard_map/ppermute | solution.py:298
  182.8 0.8 copy-start.8
  182.8 0.9 copy-start.9
  182.8 1.1 copy-start.10
  241.6 21.0 %copy-start = (f32[16,64,128]{2,1,0:T(8,128)S(1)}, f32[16,64,128]{2,1,0:T(8,128)}, u32[]{:S(2)}) copy-start(f32[16,64,128]{2,1,0:T(8,128)} %get-tuple-element.13) | copy-start | bytes 1572868
  241.6 2.7 %collective-permute-start.21 = (bf16[4,16,64,128]{3,2,1,0:T(8,128)(2,1)S(1)}, bf16[4,16,64,128]{3,2,1,0:T(8,128)(2,1)S(1)}, u32[]{:S(2)}, u32[]{:S(2)}) collective-permute-start(bf16[4,16,64,128]{3,2,1,0:T(8,128)(2,1)S(1)} %slice.79), channel_id=1, source_target_pairs={{0,1},{1,0},{2,3},{3,2},{4,5},{5,4},{6,7},{7,6},{8,9},{9,8},{10,11... | collective-permute-start | bytes 3145736 | tf_op jit(solution)/shard_map/ppermute | solution.py:283
  244.8 14.3 %collective-permute-start.22 = (bf16[16,64,128]{2,1,0:T(8,128)(2,1)S(1)}, bf16[16,64,128]{2,1,0:T(8,128)(2,1)S(1)}, u32[]{:S(2)}, u32[]{:S(2)}) collective-permute-start(bf16[16,64,128]{2,1,0:T(8,128)(2,1)S(1)} %get-tuple-element.21), channel_id=1, source_target_pairs={{0,6},{1,7},{2,0},{3,1},{4,2},{5,3},{6,4},{7,5},{8,14},{9,15},{10,... | collective-permute-start | bytes 786440 | tf_op jit(solution)/shard_map/ppermute | solution.py:280
  247.6 14.9 %collective-permute-start.23 = (bf16[16,64,128]{2,1,0:T(8,128)(2,1)S(1)}, bf16[16,64,128]{2,1,0:T(8,128)(2,1)S(1)}, u32[]{:S(2)}, u32[]{:S(2)}) collective-permute-start(bf16[16,64,128]{2,1,0:T(8,128)(2,1)S(1)} %get-tuple-element.23), channel_id=1, source_target_pairs={{0,2},{1,3},{2,4},{3,5},{4,6},{5,7},{6,0},{7,1},{8,10},{9,11},{10,... | collective-permute-start | bytes 786440 | tf_op jit(solution)/shard_map/ppermute | solution.py:280
  247.6 14.9 %collective-permute-start.24 = (bf16[16,64,128]{2,1,0:T(8,128)(2,1)S(1)}, bf16[16,64,128]{2,1,0:T(8,128)(2,1)S(1)}, u32[]{:S(2)}, u32[]{:S(2)}) collective-permute-start(bf16[16,64,128]{2,1,0:T(8,128)(2,1)S(1)} %get-tuple-element.22), channel_id=1, source_target_pairs={{0,4},{1,5},{2,6},{3,7},{4,0},{5,1},{6,2},{7,3},{8,12},{9,13},{10,... | collective-permute-start | bytes 786440 | tf_op jit(solution)/shard_map/ppermute | solution.py:280
Sparse Core Ops, SparseCore 0:
  12.1 108.7 all-gather.1
